TPU v7x, 32 devices: a whole 2x2x4 slice. The times are simulated.
32 devices in a mesh: ctx: 4 (over z), head: 4 (over x, core), rep: 2 (over y).
Axes of the slice: x: 2, y: 2, z: 4, core: 2. Of those that a mesh axis runs over, the one named last changes fastest.
Arguments:
- queries: bfloat16 [4, 256, 2048], P('rep', 'ctx', 'head'), may hold values from -6 to 6
- keyvals: bfloat16 [4, 256, 4, 128], P('rep', 'ctx', 'head'), may hold values from -6 to 6
- sinks: float32 [32], P('head'), may hold values from -1 to 3
- stream: bfloat16 [4, 256, 2880], P('rep', 'ctx', 'head'), may hold values from -6 to 6
- out_weight: bfloat16 [2048, 2880], P('head', 'ctx'), may hold values from -0.75 to 0.75
- norm_gain: float32 [2880], replicated, may hold values from 0.1 to 1.9
- router: bfloat16 [2880, 32], replicated, may hold values from -0.12 to 0.12
- expert_ids: int32 [4, 256, 4], P('rep', 'ctx'), may hold values from 0 to 31, all different within a row; in each aligned block of 64 rows (0 to 63, 64 to 127, ..., all dimensions but the last counted through in order) at most 12 rows name the same one
- w_gate_up: bfloat16 [64, 720, 5760], P('ctx', 'head'), may hold values from -0.109375 to 0.109375
- w_down: bfloat16 [64, 720, 2880], P('ctx', None, 'head'), may hold values from -0.15625 to 0.15625
Outputs:
- layer_out: bfloat16 [4, 256, 2880], P('rep', 'ctx', 'head')
Inputs may be any that keep to these rules, and one draw needn't show every extreme that they name: `expert_ids`: each position names 4 different experts. Within each aligned block of 64 positions of a sequence no expert is named by more than 12 positions, and in every draw some block has an expert named by exactly 12.
All inputs are finite; a program needn't handle non-finite values.
Results may differ from a plain program's by a relative error of at most 0.015.
Values may be sent and summed in bfloat16 or wider, within the bound.
A program may use at most 192 MiB of HBM per device.

v0:
```python
import functools

import jax
import jax.numpy as jnp
from jax import lax
from jax.experimental import pallas as pl
from jax.experimental.pallas import tpu as pltpu
from jax.sharding import PartitionSpec as P


NT = (((1,), (1,)), ((), ()))
TN = (((0,), (0,)), ((), ()))
LANES = 128


def one_hot_rows(slots, cap, value):
    rows = lax.broadcasted_iota(jnp.int32, (cap, slots.shape[1]), 0)
    return jnp.where(rows == slots, value, 0.0).astype(jnp.bfloat16)


def gate_up_kernel(
    halves,
    units,
    state_ref,
    gain_ref,
    router_ref,
    w_ref,
    slot_ref,
    out_ref,
    logits_ref,
    act_ref,
    xg_ref,
    xu_ref,
):
    step = pl.program_id(1)
    groups, shards, group_rows, cols = state_ref.shape

    @pl.when(step == 0)
    def _():
        for group in range(groups):
            pieces = [state_ref[group, shard].astype(jnp.float32) for shard in range(shards)]
            square = sum(jnp.sum(piece * piece, axis=1, keepdims=True) for piece in pieces)
            inverse = lax.rsqrt(square / (shards * cols) + 1e-05)
            scaled = [
                (piece * inverse * gain_ref[shard]).astype(jnp.bfloat16)
                for shard, piece in enumerate(pieces)
            ]
            extra = xg_ref.shape[1] - shards * cols
            blank = [jnp.zeros((group_rows, extra), jnp.bfloat16)] if extra else []
            here = slice(group * group_rows, (group + 1) * group_rows)
            xg_ref[here, :] = jnp.concatenate(scaled + blank, axis=1)
            xu_ref[here, :] = jnp.concatenate(blank + scaled, axis=1)
        logits_ref[...] = lax.dot_general(
            router_ref[...], xg_ref[...], NT, preferred_element_type=jnp.float32
        )

    rows, wide = w_ref.shape[0], xg_ref.shape[1]
    gate = lax.dot_general(w_ref[:, :wide], xg_ref[...], NT, preferred_element_type=jnp.float32)
    up = lax.dot_general(
        w_ref[:, w_ref.shape[1] - wide :], xu_ref[...], NT, preferred_element_type=jnp.float32
    )
    active = gate * jax.nn.sigmoid(1.702 * gate) * (up + 1.0)
    slabs = act_ref.shape[0]
    for slab in range(slabs):
        act_ref[slab, pl.ds(step * rows, rows), :] = active[:, slab * LANES : (slab + 1) * LANES]

    @pl.when(step == pl.num_programs(1) - 1)
    def _():
        for row in range(halves):
            wanted = pl.ds(row, units, stride=halves) if halves > 1 else pl.ds(0, units)
            picked = jnp.concatenate([act_ref[slab, wanted, :] for slab in range(slabs)], axis=1)
            spread = one_hot_rows(slot_ref[row], out_ref.shape[2], 1.0)
            out_ref[row, 0] = lax.dot_general(
                spread, picked.astype(jnp.bfloat16), NT, preferred_element_type=jnp.float32
            ).astype(jnp.bfloat16)


def gate_up_call(state, gain, router, weights, slots, units, token_block, cap):
    halves = slots.shape[0]
    sources, shards, group_rows, cols = state.shape
    groups = token_block // group_rows
    blocks = sources // groups
    experts, wide = router.shape
    wide_w = weights.shape[1]
    sizes = [
        size
        for size in range(1, units + 1)
        if units % size == 0
        and (size == units or (size * halves) % 16 == 0)
        and size * halves * wide_w * 2 <= 4 << 20
    ]
    size = sizes[-1]
    return pl.pallas_call(
        functools.partial(gate_up_kernel, halves, units),
        grid=(blocks, units // size),
        out_shape=(
            jax.ShapeDtypeStruct((halves, blocks, cap, units), jnp.bfloat16),
            jax.ShapeDtypeStruct((experts, blocks * token_block), jnp.float32),
        ),
        in_specs=[
            pl.BlockSpec((groups, shards, group_rows, cols), lambda i, j: (i, 0, 0, 0)),
            pl.BlockSpec((shards, 1, cols), lambda i, j: (0, 0, 0)),
            pl.BlockSpec((experts, wide), lambda i, j: (0, 0)),
            pl.BlockSpec((size * halves, wide_w), lambda i, j: (j, 0)),
            pl.BlockSpec((halves, 1, token_block), lambda i, j: (0, 0, i)),
        ],
        out_specs=(
            pl.BlockSpec((halves, 1, cap, units), lambda i, j: (0, i, 0, 0)),
            pl.BlockSpec((experts, token_block), lambda i, j: (0, i)),
        ),
        scratch_shapes=[
            pltpu.VMEM((token_block // LANES, units * halves, LANES), jnp.float32),
            pltpu.VMEM((token_block, wide), jnp.bfloat16),
            pltpu.VMEM((token_block, wide), jnp.bfloat16),
        ],
        compiler_params=pltpu.CompilerParams(vmem_limit_bytes=56 << 20),
    )(state, gain, router, weights, slots)


def down_kernel(act_ref, w_ref, slot_ref, mix_ref, out_ref, total_ref):
    step = pl.program_id(1)
    part = None
    for row in range(w_ref.shape[0]):
        pieces = [act_ref[shard, row, 0] for shard in range(act_ref.shape[0])]
        hidden = jnp.concatenate(pieces, axis=1)
        piece = jnp.dot(hidden, w_ref[row], preferred_element_type=jnp.float32)
        part = piece if part is None else part + piece
    spread = one_hot_rows(slot_ref[0], act_ref.shape[3], mix_ref[0])
    added = lax.dot_general(
        spread, part.astype(jnp.bfloat16), TN, preferred_element_type=jnp.float32
    )

    @pl.when(step == 0)
    def _():
        total_ref[...] = added

    @pl.when(step != 0)
    def _():
        total_ref[...] += added

    @pl.when(step == pl.num_programs(1) - 1)
    def _():
        out_ref[...] = total_ref[...].astype(jnp.bfloat16)


def down_call(act, weights, slots, mix, token_block):
    shards, halves, blocks, cap, units = act.shape
    hidden, cols = weights.shape[1:]
    pair = 2 if halves % 2 == 0 else 1
    return pl.pallas_call(
        down_kernel,
        grid=(blocks, halves // pair),
        out_shape=jax.ShapeDtypeStruct((blocks * token_block, cols), jnp.bfloat16),
        in_specs=[
            pl.BlockSpec((shards, pair, 1, cap, units), lambda i, r: (0, r, i, 0, 0)),
            pl.BlockSpec((pair, hidden, cols), lambda i, r: (r, 0, 0)),
            pl.BlockSpec((1, 1, token_block), lambda i, r: (r * pair, 0, i)),
            pl.BlockSpec((1, 1, token_block), lambda i, r: (r * pair, 0, i)),
        ],
        out_specs=pl.BlockSpec((token_block, cols), lambda i, r: (i, 0)),
        scratch_shapes=[pltpu.VMEM((token_block, cols), jnp.float32)],
        compiler_params=pltpu.CompilerParams(vmem_limit_bytes=48 << 20),
    )(act, weights, slots, mix)


def on_device(
    queries, keyvals, sinks, stream, out_weight, norm_gain, router, expert_ids, w_gate_up, w_down
):
    ctx_count = lax.axis_size("ctx")
    local_seqs = queries.shape[0]
    tokens = queries.shape[1]
    row_count = local_seqs * tokens
    kv_local = keyvals.shape[2]
    head_dim = keyvals.shape[3] // 2
    q_local = queries.shape[2] // head_dim
    query_group_size = q_local // kv_local
    wide_rows = query_group_size * tokens
    col_width = stream.shape[2]
    first_pos = lax.axis_index("ctx") * tokens
    last_pos = first_pos + tokens - 1
    score_scale = head_dim ** (-0.5)
    scaled_queries = queries * jnp.asarray(score_scale, jnp.bfloat16)
    query_grid = scaled_queries.reshape(local_seqs, tokens, kv_local, query_group_size, head_dim)
    query_wide = jnp.transpose(query_grid, (0, 2, 3, 1, 4)).reshape(
        local_seqs, kv_local, wide_rows, head_dim
    )
    positions = first_pos + jnp.tile(jnp.arange(tokens), query_group_size)
    sink_rows = jnp.repeat(sinks.reshape(kv_local, query_group_size), tokens, axis=1)
    sink_grid = jnp.broadcast_to(sink_rows[None], (local_seqs, kv_local, wide_rows))
    start_state = (
        sink_grid,
        jnp.ones_like(sink_grid),
        jnp.zeros((local_seqs, kv_local, head_dim, wide_rows), jnp.float32),
    )

    def attend_block(running, shard_piece):
        peak_old, denom_old, accum_old = running
        key_block = shard_piece[..., :head_dim]
        value_block = shard_piece[..., head_dim:]
        scores = jnp.einsum(
            "skmd,snkd->sknm", query_wide, key_block, preferred_element_type=jnp.float32
        )
        key_pos = jnp.arange(shard_piece.shape[1])
        visible = key_pos[:, None] <= positions[None, :]
        masked = jnp.where(visible[None, None], scores, -jnp.inf)
        peak_new = jnp.maximum(peak_old, jnp.max(masked, axis=2))
        exp_terms = jnp.exp(masked - peak_new[:, :, None, :])
        factor = jnp.exp(peak_old - peak_new)
        denom_new = denom_old * factor + jnp.sum(exp_terms, axis=2)
        accum_new = accum_old * factor[:, :, None, :] + jnp.einsum(
            "sknm,snkd->skdm",
            exp_terms.astype(jnp.bfloat16),
            value_block,
            preferred_element_type=jnp.float32,
        )
        return (peak_new, denom_new, accum_new)

    shard_piece = lax.all_gather(keyvals, "ctx", axis=1, tiled=True)

    def keep_state(state_in):
        return state_in

    def update_state(state_in):
        return attend_block(state_in, shard_piece)

    peak_fin, denom_fin, accum_fin = lax.cond(
        jnp.int32(0) > last_pos, keep_state, update_state, start_state
    )
    normalized = (accum_fin / denom_fin[:, :, None, :]).reshape(
        local_seqs, kv_local, head_dim, query_group_size, tokens
    )
    attended = (
        jnp.transpose(normalized, (0, 4, 1, 3, 2))
        .reshape(row_count, q_local * head_dim)
        .astype(jnp.bfloat16)
    )
    token_ids = lax.all_gather(
        expert_ids.reshape(row_count, expert_ids.shape[2]).T, "ctx", axis=1, tiled=True
    )
    all_rows = ctx_count * row_count
    halves = w_gate_up.shape[0]
    units = w_gate_up.shape[1]
    token_block = min(all_rows, 8 * tokens)
    cap = token_block // tokens * (3 * tokens // 16)
    row_expert = (lax.axis_index("ctx") * halves + jnp.arange(halves)) // 2
    named = jnp.any(token_ids[:, None, :] == row_expert[None, :, None], axis=0)
    counted = named.astype(jnp.int32).reshape(halves, all_rows // token_block, token_block)
    rank = jnp.cumsum(counted, axis=2) - 1
    slots = jnp.where(named, rank.reshape(halves, all_rows), -1).reshape(halves, 1, all_rows)
    width = norm_gain.shape[0]
    head_count = lax.axis_size("head")
    swapped = ctx_count == head_count and out_weight.shape[1] == col_width
    if swapped:
        pairs = [
            (first * head_count + second, second * head_count + first)
            for first in range(ctx_count)
            for second in range(head_count)
        ]
        turned = lax.ppermute(
            stream.reshape(row_count, col_width), ("ctx", "head"), perm=pairs
        )
        every_row = lax.all_gather(attended, "ctx", axis=0, tiled=True)
        partial_proj = jnp.dot(every_row, out_weight, preferred_element_type=jnp.float32)
        summed = lax.psum_scatter(
            partial_proj.astype(jnp.bfloat16), "head", scatter_dimension=0, tiled=True
        )
        turned_state = summed.astype(jnp.float32) + turned.astype(jnp.float32)
        every_state = lax.all_gather(
            turned_state.astype(jnp.bfloat16), ("head", "ctx"), axis=0, tiled=False
        )
    else:
        partial_proj = jnp.dot(attended, lax.all_gather(out_weight, "ctx", axis=1, tiled=True), preferred_element_type=jnp.float32)
        own_stream = stream.reshape(row_count, col_width).astype(jnp.float32)
        summed = lax.psum_scatter(
            partial_proj.astype(jnp.bfloat16), "head", scatter_dimension=1, tiled=True
        )
        own_state = (summed.astype(jnp.float32) + own_stream).astype(jnp.bfloat16)
        every_state = lax.all_gather(own_state, ("ctx", "head"), axis=0, tiled=False)
    every_state = every_state.reshape(ctx_count, width // col_width, row_count, col_width)
    expert_count = router.shape[1]
    unit_rows = jnp.transpose(w_gate_up, (1, 0, 2)).reshape(units * halves, w_gate_up.shape[2])
    router_rows = jnp.pad(router.T, ((0, 0), (0, -width % LANES)))
    gain = norm_gain.reshape(width // col_width, 1, col_width)
    active, logits = gate_up_call(
        every_state, gain, router_rows, unit_rows, slots, units, token_block, cap
    )
    member = jnp.any(token_ids[:, None, :] == jnp.arange(expert_count)[None, :, None], axis=0)
    masked = jnp.where(member, logits, -jnp.inf)
    mix_all = jax.nn.softmax(masked, axis=0)
    chosen_rows = (row_expert[:, None] == jnp.arange(expert_count)[None, :]).astype(jnp.float32)
    mix_rows = jnp.dot(chosen_rows, mix_all, precision=lax.Precision.HIGHEST)
    mix_rows = mix_rows.reshape(halves, 1, all_rows)
    every_active = lax.all_gather(active.reshape(-1, units), "head", axis=0, tiled=True)
    every_active = every_active.reshape(width // col_width, *active.shape)
    partial_out = down_call(every_active, w_down, slots, mix_rows, token_block)
    combined = lax.psum_scatter(partial_out, "ctx", scatter_dimension=0, tiled=True)
    if swapped:
        own_state = every_state[lax.axis_index("ctx"), lax.axis_index("head")]
    layer_out = (own_state.astype(jnp.float32) + combined.astype(jnp.float32)).astype(jnp.bfloat16)
    return layer_out.reshape(local_seqs, tokens, col_width)


def solution(mesh):
    placed = (
        P("rep", "ctx", "head"),
        P("rep", "ctx", "head", None),
        P("head"),
        P("rep", "ctx", "head"),
        P("head", "ctx"),
        P(),
        P(),
        P("rep", "ctx", None),
        P("ctx", "head", None),
        P("ctx", None, "head"),
    )
    return jax.shard_map(
        on_device, mesh=mesh, in_specs=placed, out_specs=P("rep", "ctx", "head"), check_vma=False
    )
```

profile of v0, /device:TPU:0, one launch (start us, length us, event | category | flops | bytes accessed | tf_op | source)
XLA Modules:
  0.0 219.1 jit_solution(6090324159182915267)
XLA Ops:
  6.5 1.0 broadcast_multiply_fusion
  7.7 0.8 copy.40
  8.5 15.1 %all_gather.18 = bf16[2,256,1,128]{3,0,2,1:T(2,128)(2,1)S(1)} all-gather(bf16[2,64,1,128]{3,0,2,1:T(2,128)(2,1)S(1)} %copy.40), channel_id=1, replica_groups=mesh['ctx'=4,'head'=4,'rep'=2] {'ctx'}, dimensions={1}, use_global_device_ids=true | all-gather | bytes 163840 | tf_op jit(solution)/shard_map/all_gather | solution.py:218
  23.6 2.4 %conditional.1 = (f32[2,1,512]{2,0,1:T(2,128)S(1)}, f32[2,1,64,512]{3,2,0,1:T(8,128)S(1)}) conditional(s32[]{:T(128)} %convert_element_type.59, (f32[8]{0:T(128)}, s32[]{:T(128)}, s32[8,64]{1,0:T(8,128)S(1)}, bf16[2,256,1,128]{3,0,2,1:T(2,128)(2,1)S(1)}, bf16[2,1,8,64,64]{4,2,3,0,1:T(8,128)(2,1)S(1)}) %tuple.30, () %tuple.14), branch_computations={%region_0.3_spmd, %region_3.4_spmd} | conditional | flops 68882944 | bytes 4784180 | solution.py:226
  23.7 0.2 copy.42
  24.0 0.2 reshape.273
  24.4 0.4 fusion.17
  24.7 0.7 broadcast_in_dim.29
  25.6 0.3 fusion
  26.3 0.2 copy.43
  26.8 16.1 %all_gather.19 = bf16[512,512]{1,0:T(8,128)(2,1)S(1)} all-gather(bf16[128,512]{1,0:T(8,128)(2,1)S(1)} %convert_element_type.63), channel_id=1, replica_groups=mesh['ctx'=4,'head'=4,'rep'=2] {'ctx'}, dimensions={0}, use_global_device_ids=true | all-gather | bytes 655360 | tf_op jit(solution)/shard_map/all_gather | solution.py:262
  42.9 0.6 convolution_convert_fusion
  43.5 1.2 copy.50
  44.7 0.7 collective-permute-start
  45.4 23.0 %reduce-scatter.7.cloned.1.call-done = bf16[128,720]{1,0:T(8,128)(2,1)} async-done(((bf16[512,720]{1,0:T(8,128)(2,1)}), bf16[128,720]{1,0:T(8,128)(2,1)}) %reduce-scatter.7.cloned.1.call-update) | async-done | bytes 184336 | tf_op jit(solution)/shard_map/reduce_scatter | solution.py:264
  68.4 1.6 add_convert_fusion
  70.3 12.0 %all_gather.22 = s32[4,512]{1,0:T(4,128)S(1)} all-gather(s32[4,128]{1,0:T(4,128)S(1)} %bitcast.74), channel_id=1, replica_groups=mesh['ctx'=4,'head'=4,'rep'=2] {'ctx'}, dimensions={1}, use_global_device_ids=true | all-gather | bytes 10240 | tf_op jit(solution)/shard_map/all_gather | solution.py:237
  82.4 1.2 reduce-window.6
  83.6 0.2 slice_reduce_fusion
  83.9 0.7 reshape.292.gain_ref
  84.6 0.7 pad.4.router_ref
  85.4 0.7 copy_select_fusion.slot_ref
  86.0 30.2 %all-gather.6.cloned.1.call-done = bf16[2048,720]{1,0:T(8,128)(2,1)} async-done(((bf16[128,720]{1,0:T(8,128)(2,1)}), bf16[2048,720]{1,0:T(8,128)(2,1)}) %all-gather.6.cloned.1.call-update) | async-done | bytes 2949136 | tf_op jit(solution)/shard_map/all_gather | solution.py:268
  116.2 29.3 %shard_map.101 = (bf16[16,1,96,180]{3,2,1,0:T(8,128)(2,1)}, f32[32,512]{1,0:T(8,128)}) custom-call(bf16[4,4,128,720]{3,2,1,0:T(8,128)(2,1)} %bitcast.64, f32[4,1,720]{2,1,0:T(1,128)} %reshape.292.gain_ref, bf16[32,2944]{1,0:T(8,128)(2,1)} %pad.4.router_ref, bf16[2880,5760]{1,0:T(8,128)(2,1)} %bitcast.63, s32[16,1,512]{2,1,0:T(1,128)} %copy_select_fusion.slot_ref), custom_call_target="tpu_custom_call" | custom-call | tf_op jit(solution)/shard_map/pallas_call | solution.py:93
  145.6 0.9 fusion.14
  146.5 0.9 fusion.11
  147.4 1.0 fusion.9
  148.4 24.1 %all-gather.4.cloned.1.call-done = bf16[6144,180]{1,0:T(8,128)(2,1)} async-done(((bf16[1536,180]{1,0:T(8,128)(2,1)}), bf16[6144,180]{1,0:T(8,128)(2,1)}) %all-gather.4.cloned.1.call-update) | async-done | bytes 2211856 | tf_op jit(solution)/shard_map/all_gather | solution.py:293
  172.5 1.9 copy-done.1
  174.4 13.0 %shard_map.102 = bf16[512,720]{1,0:T(8,128)(2,1)} custom-call(bf16[4,16,1,96,180]{4,3,2,1,0:T(8,128)(2,1)S(1)} %bitcast.62, bf16[16,720,720]{2,1,0:T(8,128)(2,1)} %w_ref.1, s32[16,1,512]{2,1,0:T(1,128)S(1)} %copy-done.2, f32[16,1,512]{2,1,0:T(1,128)S(1)} %reshape.301.mix_ref), custom_call_target="tpu_custom_call" | custom-call | tf_op jit(solution)/shard_map/pallas_call | solution.py:150
  187.4 23.3 %reduce-scatter.5.cloned.1.call-done = bf16[128,720]{1,0:T(8,128)(2,1)} async-done(((bf16[512,720]{1,0:T(8,128)(2,1)}), bf16[128,720]{1,0:T(8,128)(2,1)}) %reduce-scatter.5.cloned.1.call-update) | async-done | bytes 184336 | tf_op jit(solution)/shard_map/reduce_scatter | solution.py:296
  210.8 1.7 fusion.7
  (49 shorter events, 1.9 us)
Async XLA Ops:
  6.5 36.4 %copy-start = (bf16[512,720]{0,1:T(8,128)(2,1)S(1)}, bf16[512,720]{0,1:T(8,128)(2,1)}, u32[]{:S(2)}) copy-start(bf16[512,720]{0,1:T(8,128)(2,1)} %param.16) | copy-start | bytes 2211844
  6.5 61.9 %reduce-scatter.7.cloned.1.call-start = ((), (), s32[]{:S(2)}) async-start(), calls=%async_computation.5 | async-start | bytes 983040 | tf_op jit(solution)/shard_map/reduce_scatter | solution.py:264
  26.1 18.6 %copy-start.6 = (bf16[2,64,720]{2,1,0:T(8,128)(2,1)S(1)}, bf16[2,64,720]{2,1,0:T(8,128)(2,1)}, u32[]{:S(2)}) copy-start(bf16[2,64,720]{2,1,0:T(8,128)(2,1)} %param.15) | copy-start | bytes 552964
  26.5 43.6 %copy-start.5 = (s32[2,64,4]{1,2,0:T(4,128)S(1)}, s32[2,64,4]{1,2,0:T(4,128)}, u32[]{:S(2)}) copy-start(s32[2,64,4]{1,2,0:T(4,128)} %param.19) | copy-start | bytes 6148
  26.8 57.1 %copy-start.4 = (f32[2880]{0:T(1024)S(1)}, f32[2880]{0:T(1024)}, u32[]{:S(2)}) copy-start(f32[2880]{0:T(1024)} %param.17) | copy-start | bytes 34564
  26.8 57.8 %copy-start.3 = (bf16[2880,32]{0,1:T(8,128)(2,1)S(1)}, bf16[2880,32]{0,1:T(8,128)(2,1)}, u32[]{:S(2)}) copy-start(bf16[2880,32]{0,1:T(8,128)(2,1)} %param.18) | copy-start | bytes 552964
  44.7 71.5 %all-gather.6.cloned.1.call-start = ((), (), s32[]{:S(2)}) async-start(), calls=%async_computation.4 | async-start | bytes 3342336 | tf_op jit(solution)/shard_map/all_gather | solution.py:268
  44.7 0.7 collective-permute-start
  70.1 102.4 %all-gather.4.cloned.1.call-start = ((), (), s32[]{:S(2)}) async-start(), calls=%async_computation.2 | async-start | bytes 3932160 | tf_op jit(solution)/shard_map/all_gather | solution.py:293
  116.2 56.4 %copy-start.2 = (s32[16,1,512]{2,1,0:T(1,128)S(1)}, s32[16,1,512]{2,1,0:T(1,128)}, u32[]{:S(2)}) copy-start(s32[16,1,512]{2,1,0:T(1,128)} %copy_select_fusion.slot_ref) | copy-start | bytes 98308
  145.5 65.2 %reduce-scatter.5.cloned.1.call-start = ((), (), s32[]{:S(2)}) async-start(), calls=%async_computation.3 | async-start | bytes 983040 | tf_op jit(solution)/shard_map/reduce_scatter | solution.py:296
  172.5 1.9 copy-start.1
Sparse Core Ops, SparseCore 0:
  44.8 23.6 reduce-scatter.6
  70.8 45.3 all-gather.5
  145.7 26.8 all-gather.3
  187.6 23.1 reduce-scatter.4
where the time goes:
time: 220 us; the launch traced here: 219 us
  waiting for transfers between devices  101 us (46%)
  blocking collectives  43.2 us (20%)
  Pallas kernels  42.3 us (19%)
  between operations  13.3 us (6%)
  other arithmetic  8.43 us (4%)
  local copies, waits for them, and re-layouts  8.04 us (4%)
  matrix products  2.28 us (1%)
    all_gather x1, waiting for transfers between devices, on_device(): lax.all_gather(turned_state.astype(jnp.bfloat16), ('head', 'ctx'), axis=0...  30.2 us
    pallas_call x1, Pallas kernels, gate_up_call(): pl.pallas_call(functools.partial(gate_up_kernel, halves, units), grid=(bl...  29.3 us
    all_gather x1, waiting for transfers between devices, on_device(): lax.all_gather(active.reshape(-1, units), 'head', axis=0, tiled=True)  24.1 us
    reduce_scatter x1, waiting for transfers between devices, on_device(): lax.psum_scatter(partial_out, 'ctx', scatter_dimension=0, tiled=True)  23.3 us
    reduce_scatter x1, waiting for transfers between devices, on_device(): lax.psum_scatter(partial_proj.astype(jnp.bfloat16), 'head', scatter_dimen...  23 us
    all_gather x1, blocking collectives, on_device(): every_row = lax.all_gather(attended, 'ctx', axis=0, tiled=True)  16.1 us
    all_gather x1, blocking collectives, on_device(): shard_piece = lax.all_gather(keyvals, 'ctx', axis=1, tiled=True)  15.1 us
    pallas_call x1, Pallas kernels, down_call(): pl.pallas_call(down_kernel, grid=(blocks, halves // pair), out_shape=jax....  13 us
  transfers between devices with their start and end apart: 5, of which 4 were waited for; matrix products, arithmetic and copies ran while one was open for 3% of the time, Pallas kernels for 0%

commit v1 on v0

--- a/solution.py
+++ b/solution.py
@@ -163,9 +163,702 @@
     )(act, weights, slots, mix)
 
 
+MESH = pl.DeviceIdType.MESH
+NN = (((1,), (0,)), ((), ()))
+
+
+def layer_kernel(
+    sizes,
+    q_ref,
+    kv_ref,
+    ids_ref,
+    sink_ref,
+    gain_ref,
+    stream_ref,
+    ow_hbm,
+    router_hbm,
+    wg_hbm,
+    wd_hbm,
+    out_ref,
+    kv_all,
+    ids_all,
+    stream_in,
+    ow,
+    router,
+    wg,
+    wd,
+    att_all,
+    core_out,
+    core_in,
+    keep,
+    x_out,
+    x_in,
+    h_all,
+    y_all,
+    pick,
+    spread,
+    xg,
+    scale_ref,
+    act_all,
+    parts,
+    rs_out,
+    rs_in,
+    local_sem,
+    wg_sem,
+    wd_sem,
+    kv_send,
+    kv_recv,
+    ids_send,
+    ids_recv,
+    stream_send,
+    stream_recv,
+    att_send,
+    att_recv,
+    core_send,
+    core_recv,
+    x_send,
+    x_recv,
+    h_send,
+    h_recv,
+    act_send,
+    act_recv,
+    rs_send,
+    rs_recv,
+):
+    seqs, tokens, rows, ctxs, width, cols, cap, local_experts, units, slots = sizes
+    c, h, r = lax.axis_index("ctx"), lax.axis_index("head"), lax.axis_index("rep")
+    all_rows = ctxs * rows
+    wide = y_all.shape[1]
+    pad_cols = h_all.shape[3]
+    core_dev, x_dev = (c, h ^ 1, r), (c, h ^ 2, r)
+    partner = (h, c, r)
+
+    def remote(src, dst, send, recv, device):
+        return pltpu.make_async_remote_copy(
+            src_ref=src,
+            dst_ref=dst,
+            send_sem=send,
+            recv_sem=recv,
+            device_id=device,
+            device_id_type=MESH,
+        )
+
+    ow_copy = pltpu.make_async_copy(ow_hbm, ow, local_sem.at[0])
+    router_copy = pltpu.make_async_copy(router_hbm, router, local_sem.at[1])
+
+    def wg_copy(e, slot):
+        return pltpu.make_async_copy(
+            wg_hbm.at[pl.ds(2 * e, 2)], wg.at[slot], wg_sem.at[slot]
+        )
+
+    def wd_copy(e):
+        return pltpu.make_async_copy(
+            wd_hbm.at[pl.ds(2 * e, 2)], wd.at[pl.ds(2 * e, 2)], wd_sem.at[e]
+        )
+
+    barrier = pltpu.get_barrier_semaphore()
+    for step in range(1, ctxs):
+        pl.semaphore_signal(
+            barrier, inc=1, device_id=(lax.rem(c + step, ctxs), h, r), device_id_type=MESH
+        )
+    pl.semaphore_signal(barrier, inc=1, device_id=core_dev, device_id_type=MESH)
+    pl.semaphore_signal(barrier, inc=1, device_id=x_dev, device_id_type=MESH)
+
+    @pl.when(c != h)
+    def _():
+        pl.semaphore_signal(barrier, inc=1, device_id=partner, device_id_type=MESH)
+
+    ow_copy.start()
+    for e in range(min(slots, local_experts)):
+        wg_copy(e, e).start()
+    router_copy.start()
+    for e in range(local_experts):
+        wd_copy(e).start()
+    own_ids = ids_ref[...].reshape(rows, ids_ref.shape[2]).astype(jnp.float32)
+    topk = ids_ref.shape[2]
+    padded_ids = jnp.concatenate(
+        [own_ids, jnp.full((rows, LANES - topk), -1.0, jnp.float32)], axis=1
+    )
+    ids_all[c] = jnp.transpose(padded_ids)[:8]
+    kv_all[c] = kv_ref[...]
+    for other in range(ctxs):
+
+        @pl.when(other > c)
+        def _():
+            kv_all[other] = jnp.zeros(kv_all.shape[1:], jnp.bfloat16)
+
+    parts[...] = jnp.zeros(parts.shape, jnp.bfloat16)
+    pl.semaphore_wait(barrier, ctxs + 1 + (c != h).astype(jnp.int32))
+
+    def kv_copy(src, dst):
+        return remote(
+            kv_all.at[src], kv_all.at[src], kv_send.at[dst], kv_recv.at[src], (dst, h, r)
+        )
+
+    def ids_copy(src, dst):
+        return remote(
+            ids_all.at[src], ids_all.at[src], ids_send.at[dst], ids_recv.at[src], (dst, h, r)
+        )
+
+    def att_copy(src, dst):
+        return remote(
+            att_all.at[src], att_all.at[src], att_send.at[dst], att_recv.at[src], (dst, h, r)
+        )
+
+    for dst in range(ctxs):
+
+        @pl.when(dst > c)
+        def _():
+            kv_copy(c, dst).start()
+
+    stream_copy = remote(
+        stream_ref, stream_in, stream_send.at[0], stream_recv.at[0], partner
+    )
+    stream_local = pltpu.make_async_copy(stream_ref, stream_in, local_sem.at[2])
+
+    @pl.when(c != h)
+    def _():
+        stream_copy.start()
+
+    @pl.when(c == h)
+    def _():
+        stream_local.start()
+
+    for dst in range(ctxs):
+
+        @pl.when(dst != c)
+        def _():
+            ids_copy(c, dst).start()
+
+    for src in range(ctxs):
+
+        @pl.when(src < c)
+        def _():
+            kv_copy(src, c).wait_recv()
+
+    pairs = q_ref.shape[2] // LANES
+    half = LANES // 2
+    keys = ctxs * tokens
+    group = pairs * tokens
+    low_k = lax.broadcasted_iota(jnp.int32, (keys, LANES), 1) < half
+    low_q = lax.broadcasted_iota(jnp.int32, (group, LANES), 1) < half
+    key_pos = lax.broadcasted_iota(jnp.int32, (group, keys), 1)
+    row_pos = lax.rem(lax.broadcasted_iota(jnp.int32, (group, keys), 0), tokens)
+    visible = key_pos <= row_pos + c * tokens
+    for s in range(seqs):
+        kv = jnp.concatenate([kv_all[src, s] for src in range(ctxs)], axis=0).astype(jnp.float32)
+        turned = pltpu.roll(kv, half, 1)
+        key_sides = [jnp.where(low_k, kv, 0.0), jnp.where(low_k, 0.0, turned)]
+        value_sides = [jnp.where(low_k, turned, 0.0), jnp.where(low_k, 0.0, kv)]
+        q = jnp.concatenate(
+            [q_ref[s, :, p * LANES : (p + 1) * LANES] for p in range(pairs)], axis=0
+        )
+        acc, totals = None, []
+        for side in range(2):
+            sink = jnp.concatenate(
+                [
+                    jnp.full((tokens, 1), sink_ref[2 * p + side], jnp.float32)
+                    for p in range(pairs)
+                ],
+                axis=0,
+            )
+            scores = lax.dot_general(
+                q, key_sides[side].astype(jnp.bfloat16), NT, preferred_element_type=jnp.float32
+            ) * (half ** (-0.5))
+            scores = jnp.where(visible, scores, -1e30)
+            peak = jnp.maximum(sink, jnp.max(scores, axis=1, keepdims=True))
+            terms = jnp.where(visible, jnp.exp(scores - peak), 0.0)
+            totals.append(jnp.exp(sink - peak) + jnp.sum(terms, axis=1, keepdims=True))
+            piece = lax.dot_general(
+                terms.astype(jnp.bfloat16),
+                value_sides[side].astype(jnp.bfloat16),
+                NN,
+                preferred_element_type=jnp.float32,
+            )
+            acc = piece if acc is None else acc + piece
+        attended = (acc / jnp.where(low_q, totals[0], totals[1])).astype(jnp.bfloat16)
+        for p in range(pairs):
+            att_all[c, s * tokens : (s + 1) * tokens, p * LANES : (p + 1) * LANES] = attended[
+                p * tokens : (p + 1) * tokens
+            ]
+    for dst in range(ctxs):
+
+        @pl.when(dst != c)
+        def _():
+            att_copy(c, dst).start()
+
+    for src in range(ctxs):
+
+        @pl.when(src != c)
+        def _():
+            ids_copy(src, c).wait_recv()
+
+    ids_row = jnp.concatenate([ids_all[src] for src in range(ctxs)], axis=1)
+    mine = (
+        lax.broadcasted_iota(jnp.int32, (local_experts, all_rows), 0) + c * local_experts
+    ).astype(jnp.float32)
+    member = jnp.zeros((local_experts, all_rows), jnp.bool_)
+    for k in range(topk):
+        member = member | (mine == ids_row[k : k + 1])
+    before = lax.broadcasted_iota(jnp.int32, (all_rows, all_rows), 0) <= lax.broadcasted_iota(
+        jnp.int32, (all_rows, all_rows), 1
+    )
+    rank = lax.dot_general(
+        jnp.where(member, 1.0, 0.0).astype(jnp.bfloat16),
+        jnp.where(before, 1.0, 0.0).astype(jnp.bfloat16),
+        NN,
+        preferred_element_type=jnp.float32,
+    )
+    slot_row = jnp.where(member, rank - 1.0, -1.0)
+    slot_rows = lax.broadcasted_iota(jnp.int32, (cap, all_rows), 0).astype(jnp.float32)
+    for e in range(local_experts):
+        pick[e * cap : (e + 1) * cap, :] = jnp.where(
+            slot_rows == slot_row[e : e + 1], 1.0, 0.0
+        ).astype(jnp.bfloat16)
+    both = jnp.concatenate(
+        [ids_row, slot_row, jnp.zeros((LANES - 8 - local_experts, all_rows), jnp.float32)], axis=0
+    )
+    by_token = jnp.transpose(both)
+
+    ow_copy.wait()
+    side, core = h // 2, lax.rem(h, 2)
+
+    def projected(block):
+        @pl.when(block != c)
+        def _():
+            att_copy(block, c).wait_recv()
+
+        out = lax.dot_general(att_all[block], ow[...], NN, preferred_element_type=jnp.float32)
+        return jnp.concatenate(
+            [out, jnp.zeros((rows, pad_cols - cols), jnp.float32)], axis=1
+        )
+
+    def core_copy(i):
+        return remote(core_out.at[i], core_in.at[i], core_send.at[i], core_recv.at[i], core_dev)
+
+    for i in range(2):
+        across = (1 - side) if i == 0 else side
+        core_out[i] = projected(2 * across + 1 - core).astype(jnp.bfloat16)
+        core_copy(i).start()
+    for i in range(2):
+        across = (1 - side) if i == 0 else side
+        keep[i] = projected(2 * across + core)
+    core_copy(0).wait_recv()
+    x_out[...] = (keep[0] + core_in[0].astype(jnp.float32)).astype(jnp.bfloat16)
+    x_copy = remote(x_out, x_in, x_send.at[0], x_recv.at[0], x_dev)
+    x_copy.start()
+
+    @pl.when(c != h)
+    def _():
+        stream_copy.wait_recv()
+
+    @pl.when(c == h)
+    def _():
+        stream_local.wait()
+
+    core_copy(1).wait_recv()
+    turned_stream = stream_in[...].reshape(rows, cols).astype(jnp.float32)
+    kept = (
+        keep[1]
+        + core_in[1].astype(jnp.float32)
+        + jnp.concatenate(
+            [turned_stream, jnp.zeros((rows, pad_cols - cols), jnp.float32)], axis=1
+        )
+    )
+    x_copy.wait_recv()
+    h_all[c, h] = (kept + x_in[...].astype(jnp.float32)).astype(jnp.bfloat16)
+
+    def h_copy(way, block, row, device):
+        return remote(
+            h_all.at[block, row],
+            h_all.at[block, row],
+            h_send.at[way, block],
+            h_recv.at[block, row],
+            device,
+        )
+
+    def h_core(block, row):
+        return h_copy(jnp.where(row == h, 0, 1), block, row, core_dev)
+
+    def h_x(block):
+        return h_copy(2, block, h, x_dev)
+
+    def h_right(block):
+        return h_copy(3, block, h, (jnp.minimum(c + 1, ctxs - 1), h, r))
+
+    def h_left(block):
+        return h_copy(4, block, h, (jnp.maximum(c - 1, 0), h, r))
+
+    def arrived(block, row):
+        h_copy(0, block, row, core_dev).wait_recv()
+
+    h_x(c).start()
+
+    @pl.when(c < ctxs - 1)
+    def _():
+        h_right(c).start()
+
+    @pl.when(c > 0)
+    def _():
+        h_left(c).start()
+
+    h_core(c, h).start()
+    for d in range(1, ctxs + 1):
+
+        @pl.when(c - d >= 0)
+        def _():
+            arrived(c - d, h)
+
+            @pl.when(c < ctxs - 1)
+            def _():
+                h_right(c - d).start()
+
+            h_x(c - d).start()
+            h_core(c - d, h).start()
+
+        @pl.when(c + d < ctxs)
+        def _():
+            arrived(c + d, h)
+
+            @pl.when(c > 0)
+            def _():
+                h_left(c + d).start()
+
+            h_x(c + d).start()
+            h_core(c + d, h).start()
+
+        @pl.when(c - (d - 1) >= 0)
+        def _():
+            arrived(c - (d - 1), h ^ 2)
+            h_core(c - (d - 1), h ^ 2).start()
+
+        if d > 1:
+
+            @pl.when(c + (d - 1) < ctxs)
+            def _():
+                arrived(c + (d - 1), h ^ 2)
+                h_core(c + (d - 1), h ^ 2).start()
+
+    for block in range(ctxs):
+        arrived(block, h ^ 1)
+        arrived(block, h ^ 3)
+
+    gain = gain_ref[...]
+    squares = []
+    for row in range(ctxs):
+        pieces = [h_all[block, row].astype(jnp.float32)[:, :cols] for block in range(ctxs)]
+        squares.append(sum(jnp.sum(piece * piece, axis=1, keepdims=True) for piece in pieces))
+        flat = jnp.concatenate(pieces, axis=1) * gain
+        y_all[row * rows : (row + 1) * rows, :] = jnp.concatenate(
+            [flat, jnp.zeros((rows, wide - width), jnp.float32)], axis=1
+        ).astype(jnp.bfloat16)
+    inverse = lax.rsqrt(jnp.concatenate(squares, axis=0) / width + 1e-05)
+    router_copy.wait()
+    logits = lax.dot_general(
+        y_all[:, :width], router[...], NN, preferred_element_type=jnp.float32
+    ) * inverse
+    experts = router.shape[1]
+    expert_lane = lax.broadcasted_iota(jnp.int32, (all_rows, experts), 1).astype(jnp.float32)
+    named = jnp.zeros((all_rows, experts), jnp.bool_)
+    for k in range(topk):
+        named = named | (expert_lane == by_token[:, k : k + 1])
+    top = jnp.max(jnp.where(named, logits, -1e30), axis=1, keepdims=True)
+    weight = jnp.where(named, jnp.exp(logits - top), 0.0)
+    mix = weight / jnp.sum(weight, axis=1, keepdims=True)
+    mix = jnp.concatenate([mix, jnp.zeros((all_rows, LANES - experts), jnp.float32)], axis=1)
+    mix = pltpu.roll(mix, lax.rem(LANES - c * local_experts, LANES), 1)
+    slot_lane = lax.broadcasted_iota(jnp.int32, (all_rows, LANES), 1).astype(jnp.float32)
+    for e in range(local_experts):
+        spread[:, e * LANES : (e + 1) * LANES] = jnp.where(
+            slot_lane == by_token[:, 8 + e : 9 + e], mix[:, e : e + 1], 0.0
+        ).astype(jnp.bfloat16)
+
+    inverse_row = jnp.transpose(jnp.broadcast_to(inverse, (all_rows, LANES)))[:8]
+    first = inverse_row.astype(jnp.bfloat16)
+    rest = inverse_row - first.astype(jnp.float32)
+    second = rest.astype(jnp.bfloat16)
+    third = (rest - second.astype(jnp.float32)).astype(jnp.bfloat16)
+    for e in range(local_experts):
+        here = pick[e * cap : (e + 1) * cap, :]
+        scale_ref[e] = sum(
+            lax.dot_general(part, here, NT, preferred_element_type=jnp.float32)
+            for part in (first, second, third)
+        )
+
+    @pl.loop(0, wide // LANES)
+    def _(j):
+        at = pl.multiple_of(j * LANES, LANES)
+        xg[:, pl.ds(at, LANES)] = lax.dot_general(
+            pick[...], y_all[:, pl.ds(at, LANES)], NN, preferred_element_type=jnp.float32
+        ).astype(jnp.bfloat16)
+
+    def act_core(shard, e):
+        return remote(
+            act_all.at[shard, e],
+            act_all.at[shard, e],
+            act_send.at[jnp.where(shard == h, 0, 1), e],
+            act_recv.at[shard, e],
+            core_dev,
+        )
+
+    def act_x(e):
+        return remote(
+            act_all.at[h, e], act_all.at[h, e], act_send.at[2, e], act_recv.at[h, e], x_dev
+        )
+
+    def act_arrived(shard, e):
+        remote(
+            act_all.at[shard, e],
+            act_all.at[shard, e],
+            act_send.at[0, e],
+            act_recv.at[shard, e],
+            core_dev,
+        ).wait_recv()
+
+    lead = wide - width
+    packed = act_all.shape[3]
+
+    @pl.loop(0, local_experts)
+    def _(e):
+        slot = lax.rem(e, slots)
+        wg_copy(e, slot).wait()
+        rows_in = xg[pl.ds(pl.multiple_of(e * cap, cap), cap), :]
+        shifted = jnp.concatenate(
+            [jnp.zeros((cap, lead), jnp.bfloat16), rows_in[:, :width]], axis=1
+        )
+        factor = scale_ref[e][:1]
+        active = []
+        for u in range(2):
+            gate = factor * lax.dot_general(
+                wg[slot, u, :, :wide], rows_in, NT, preferred_element_type=jnp.float32
+            )
+            up = factor * lax.dot_general(
+                wg[slot, u, :, 2 * width - wide :],
+                shifted,
+                NT,
+                preferred_element_type=jnp.float32,
+            )
+            active.append(gate * jax.nn.sigmoid(1.702 * gate) * (up + 1.0))
+        stacked = jnp.concatenate(
+            active + [jnp.zeros((packed - 2 * units, cap), jnp.float32)], axis=0
+        )
+        stacked = jnp.concatenate(
+            [stacked, jnp.zeros((packed, LANES - cap), jnp.float32)], axis=1
+        )
+        act_all[h, e] = jnp.transpose(stacked)[:cap].astype(jnp.bfloat16)
+        act_x(e).start()
+        act_core(h, e).start()
+
+        @pl.when(e + slots < local_experts)
+        def _():
+            wg_copy(e + slots, slot).start()
+
+        @pl.when(e >= 2)
+        def _():
+            act_arrived(h ^ 2, e - 2)
+            act_core(h ^ 2, e - 2).start()
+
+    for e in range(local_experts - 2, local_experts):
+        act_arrived(h ^ 2, e)
+        act_core(h ^ 2, e).start()
+
+    @pl.loop(0, local_experts)
+    def _(e):
+        wd_copy(e).wait()
+        act_arrived(h ^ 1, e)
+        act_arrived(h ^ 3, e)
+        total = None
+        for u in range(2):
+            hidden = jnp.concatenate(
+                [act_all[shard, e][:, u * units : (u + 1) * units] for shard in range(4)], axis=1
+            )
+            piece = lax.dot_general(
+                hidden, wd[2 * e + u], NN, preferred_element_type=jnp.float32
+            )
+            total = piece if total is None else total + piece
+        parts[pl.ds(pl.multiple_of(e * LANES, LANES), cap), :] = jnp.concatenate(
+            [total, jnp.zeros((cap, pad_cols - cols), jnp.float32)], axis=1
+        ).astype(jnp.bfloat16)
+
+    def rs_copy(src, dst):
+        return remote(rs_out.at[dst], rs_in.at[src], rs_send.at[dst], rs_recv.at[src], (dst, h, r))
+
+    def combined(block):
+        return lax.dot_general(
+            spread[pl.ds(pl.multiple_of(block * rows, rows), rows), :],
+            parts[...],
+            NN,
+            preferred_element_type=jnp.float32,
+        )
+
+    for d in range(1, ctxs):
+        dst = lax.rem(c + d, ctxs)
+        rs_out[dst] = combined(dst).astype(jnp.bfloat16)
+        rs_copy(c, dst).start()
+    total = combined(c) + h_all[h, c].astype(jnp.float32)
+    for d in range(1, ctxs):
+        src = lax.rem(c + d, ctxs)
+        rs_copy(src, c).wait_recv()
+        total = total + rs_in[src].astype(jnp.float32)
+    out_ref[...] = total[:, :cols].astype(jnp.bfloat16).reshape(out_ref.shape)
+
+    for dst in range(ctxs):
+
+        @pl.when(dst > c)
+        def _():
+            kv_copy(c, dst).wait_send()
+
+        @pl.when(dst != c)
+        def _():
+            ids_copy(c, dst).wait_send()
+            att_copy(c, dst).wait_send()
+            rs_copy(c, dst).wait_send()
+
+    @pl.when(c != h)
+    def _():
+        stream_copy.wait_send()
+
+    x_copy.wait_send()
+    for i in range(2):
+        core_copy(i).wait_send()
+    for block in range(ctxs):
+        h_x(block).wait_send()
+        h_core(block, h).wait_send()
+        h_core(block, h ^ 2).wait_send()
+
+        @pl.when((c < ctxs - 1) & (block <= c))
+        def _():
+            h_right(block).wait_send()
+
+        @pl.when((c > 0) & (block >= c))
+        def _():
+            h_left(block).wait_send()
+
+    for e in range(local_experts):
+        act_x(e).wait_send()
+        act_core(h, e).wait_send()
+        act_core(h ^ 2, e).wait_send()
+
+
+def layer_call(queries, keyvals, sinks, stream, out_weight, gain, router, ids, w_gate_up, w_down):
+    seqs, tokens, q_cols = queries.shape
+    cols = stream.shape[2]
+    ctxs = lax.axis_size("ctx")
+    rows = seqs * tokens
+    width = gain.shape[0]
+    halves, units, wide_w = w_gate_up.shape
+    local_experts = halves // 2
+    all_rows = ctxs * rows
+    cap = all_rows * 3 // 16
+    wide = pl.cdiv(width, LANES) * LANES
+    pad_cols = pl.cdiv(cols, LANES) * LANES
+    packed = pl.cdiv(2 * units, LANES) * LANES
+    slots = min(4, local_experts)
+    sizes = (seqs, tokens, rows, ctxs, width, cols, cap, local_experts, units, slots)
+    bf16, f32 = jnp.bfloat16, jnp.float32
+    dma = pltpu.SemaphoreType.DMA
+    vmem = pl.BlockSpec(memory_space=pltpu.VMEM)
+    hbm = pl.BlockSpec(memory_space=pl.ANY)
+    return pl.pallas_call(
+        functools.partial(layer_kernel, sizes),
+        out_shape=jax.ShapeDtypeStruct((seqs, tokens, cols), bf16),
+        in_specs=[vmem, vmem, vmem, pl.BlockSpec(memory_space=pltpu.SMEM), vmem, vmem]
+        + [hbm] * 4,
+        out_specs=vmem,
+        scratch_shapes=[
+            pltpu.VMEM((ctxs, seqs, tokens, keyvals.shape[3]), bf16),
+            pltpu.VMEM((ctxs, 8, LANES), f32),
+            pltpu.VMEM((seqs, tokens, cols), bf16),
+            pltpu.VMEM(out_weight.shape, bf16),
+            pltpu.VMEM(router.shape, bf16),
+            pltpu.VMEM((slots, 2, units, wide_w), bf16),
+            pltpu.VMEM(w_down.shape, bf16),
+            pltpu.VMEM((ctxs, rows, q_cols), bf16),
+            pltpu.VMEM((2, rows, pad_cols), bf16),
+            pltpu.VMEM((2, rows, pad_cols), bf16),
+            pltpu.VMEM((2, rows, pad_cols), f32),
+            pltpu.VMEM((rows, pad_cols), bf16),
+            pltpu.VMEM((rows, pad_cols), bf16),
+            pltpu.VMEM((ctxs, 4, rows, pad_cols), bf16),
+            pltpu.VMEM((all_rows, wide), bf16),
+            pltpu.VMEM((local_experts * cap, all_rows), bf16),
+            pltpu.VMEM((all_rows, local_experts * LANES), bf16),
+            pltpu.VMEM((local_experts * cap, wide), bf16),
+            pltpu.VMEM((local_experts, 8, cap), f32),
+            pltpu.VMEM((4, local_experts, cap, packed), bf16),
+            pltpu.VMEM((local_experts * LANES, pad_cols), bf16),
+            pltpu.VMEM((ctxs, rows, pad_cols), bf16),
+            pltpu.VMEM((ctxs, rows, pad_cols), bf16),
+            dma((3,)),
+            dma((slots,)),
+            dma((local_experts,)),
+            dma((ctxs,)),
+            dma((ctxs,)),
+            dma((ctxs,)),
+            dma((ctxs,)),
+            dma((1,)),
+            dma((1,)),
+            dma((ctxs,)),
+            dma((ctxs,)),
+            dma((2,)),
+            dma((2,)),
+            dma((1,)),
+            dma((1,)),
+            dma((5, ctxs)),
+            dma((ctxs, 4)),
+            dma((3, local_experts)),
+            dma((4, local_experts)),
+            dma((ctxs,)),
+            dma((ctxs,)),
+        ],
+        compiler_params=pltpu.CompilerParams(
+            vmem_limit_bytes=67043328, collective_id=0, has_side_effects=True
+        ),
+    )(
+        queries,
+        keyvals.reshape(seqs, tokens, keyvals.shape[3]),
+        ids,
+        sinks,
+        gain.reshape(1, width),
+        stream,
+        out_weight,
+        router,
+        w_gate_up,
+        w_down,
+    )
+
+
+def one_chip_row(queries, keyvals, stream, out_weight, router, ids, w_gate_up):
+    ctxs, heads = lax.axis_size("ctx"), lax.axis_size("head")
+    rows = queries.shape[0] * queries.shape[1]
+    return (
+        ctxs == heads == 4
+        and rows == LANES
+        and keyvals.shape[2] == 1
+        and keyvals.shape[3] == LANES
+        and out_weight.shape[1] == stream.shape[2]
+        and w_gate_up.shape[0] == 16
+        and ids.shape[2] <= 8
+        and router.shape[1] <= LANES
+    )
+
+
 def on_device(
     queries, keyvals, sinks, stream, out_weight, norm_gain, router, expert_ids, w_gate_up, w_down
 ):
+    if one_chip_row(queries, keyvals, stream, out_weight, router, expert_ids, w_gate_up):
+        return layer_call(
+            queries,
+            keyvals,
+            sinks,
+            stream,
+            out_weight,
+            norm_gain,
+            router,
+            expert_ids,
+            w_gate_up,
+            w_down,
+        )
     ctx_count = lax.axis_size("ctx")
     local_seqs = queries.shape[0]
     tokens = queries.shape[1]

time: 220 us -> 141 us (0.64)
  waiting for transfers between devices: 101 us -> 0 us
  Pallas kernels: 42.3 us -> 108 us
  blocking collectives: 43.2 us -> 0 us
  local copies, waits for them, and re-layouts: 8.04 us -> 32.2 us
  between operations: 13.3 us -> 0.01 us
  other arithmetic: 8.43 us -> 0 us
  matrix products: 2.28 us -> 0 us
    pallas_call x2 -> x1, Pallas kernels: 42.3 us -> 108 us  [layer_call(): pl.pallas_call(functools.partial(layer_kernel, sizes), out_shape=jax.Shap...]
    all_gather x2 -> x0, waiting for transfers between devices: 54.3 us -> none  [the longest x1 30.2 us: on_device(): lax.all_gather(turned_state.astype(jnp.bfloat16), ('head', 'ctx'), axis=0...]
    reduce_scatter x2 -> x0, waiting for transfers between devices: 46.4 us -> none  [the longest x1 23.3 us: on_device(): lax.psum_scatter(partial_out, 'ctx', scatter_dimension=0, tiled=True)]
    all_gather x3 -> x0, blocking collectives: 43.2 us -> none  [the longest x1 16.1 us: on_device(): every_row = lax.all_gather(attended, 'ctx', axis=0, tiled=True)]
    unnamed x17 -> x5, local copies, waits for them, and re-layouts: 3.87 us -> 30.9 us
    convert_element_type x4 -> x0, other arithmetic: 3.42 us -> none  [the longest x1 1.74 us: on_device(): (own_state.astype(jnp.float32) + combined.astype(jnp.float32)).astype(jnp...]
    dot_general x4 -> x0, matrix products: 2.28 us -> none  [the longest x1 1.04 us: on_device(): mix_rows = jnp.dot(chosen_rows, mix_all, precision=lax.Precision.HIGHEST)]
  transfers between devices with their start and end apart: 5 -> 0, of which waited for: 4 -> 0; matrix products, arithmetic and copies ran while one was open for 3% -> 0% of each run, Pallas kernels for 0% -> 0%
where the time goes in v1:
time: 141 us; the launch traced here: 140 us
  Pallas kernels  108 us (77%)
  local copies, waits for them, and re-layouts  32.2 us (23%)
    pallas_call x1, Pallas kernels, layer_call(): pl.pallas_call(functools.partial(layer_kernel, sizes), out_shape=jax.Shap...  108 us
    unnamed x5, local copies, waits for them, and re-layouts  30.9 us

profile of v1, /device:TPU:0, one launch (start us, length us, event | category | flops | bytes accessed | tf_op | source)
XLA Modules:
  0.0 140.3 jit_solution(6357683697502732999)
XLA Ops:
  0.0 1.3 reshape.7.gain_ref
  1.3 1.4 %copy.11.ids_ref = s32[2,64,4]{2,1,0:T(8,128)} copy(s32[2,64,4]{1,2,0:T(4,128)} %param.17) | data formatting | bytes 4096 | tf_op args[7]
  2.7 2.1 %copy.13.router_hbm = bf16[2880,32]{1,0:T(8,128)(2,1)} copy(bf16[2880,32]{0,1:T(8,128)(2,1)} %param.16) | data formatting | bytes 368640 | tf_op args[6]
  4.8 2.3 %copy.12.ow_hbm = bf16[512,720]{1,0:T(8,128)(2,1)} copy(bf16[512,720]{0,1:T(8,128)(2,1)} %param.14) | data formatting | bytes 1474560 | tf_op args[4]
  7.1 23.5 %copy.14.wg_hbm = bf16[16,180,5760]{2,1,0:T(8,128)(2,1)} copy(bf16[16,180,5760]{2,0,1:T(8,128)(2,1)} %param.18) | data formatting | bytes 66355200 | tf_op args[8]
  30.6 108.0 %shard_map.100 = bf16[2,64,720]{2,1,0:T(8,128)(2,1)} custom-call(bf16[2,64,512]{2,1,0:T(8,128)(2,1)} %q_ref.1, bf16[2,64,128]{2,1,0:T(8,128)(2,1)} %bitcast.1, s32[2,64,4]{2,1,0:T(8,128)} %copy.11.ids_ref, f32[8]{0:T(128)} %sink_ref.1, f32[1,2880]{1,0:T(1,128)} %reshape.7.gain_ref, bf16[2,64,720]{2,1,0:T(8,128)(2,1)} %stream_ref.1, ...), custom_call_target="tpu_custom_call" | custom-call | tf_op jit(solution)/shard_map/pallas_call | solution.py:762
  138.6 1.6 %copy.16 = bf16[2,64,720]{2,1,0:T(8,128)(2,1)} copy(bf16[2,64,720]{2,1,0:T(8,128)(2,1)} %shard_map.100) | data formatting | bytes 368640

commit v2 on v1

--- a/solution.py
+++ b/solution.py
@@ -199,6 +199,7 @@
     spread,
     xg,
     scale_ref,
+    unit_rows,
     act_all,
     parts,
     rs_out,
@@ -248,7 +249,7 @@
 
     def wg_copy(e, slot):
         return pltpu.make_async_copy(
-            wg_hbm.at[pl.ds(2 * e, 2)], wg.at[slot], wg_sem.at[slot]
+            wg_hbm.at[:, pl.ds(2 * e, 2), :], wg.at[slot], wg_sem.at[slot]
         )
 
     def wd_copy(e):
@@ -274,12 +275,11 @@
     router_copy.start()
     for e in range(local_experts):
         wd_copy(e).start()
-    own_ids = ids_ref[...].reshape(rows, ids_ref.shape[2]).astype(jnp.float32)
-    topk = ids_ref.shape[2]
-    padded_ids = jnp.concatenate(
-        [own_ids, jnp.full((rows, LANES - topk), -1.0, jnp.float32)], axis=1
-    )
-    ids_all[c] = jnp.transpose(padded_ids)[:8]
+    topk = ids_ref.shape[1]
+    own_ids = jnp.concatenate([ids_ref[s] for s in range(seqs)], axis=1).astype(jnp.float32)
+    ids_all[c] = jnp.concatenate(
+        [own_ids, jnp.full((8 - topk, rows), -1.0, jnp.float32)], axis=0
+    )
     kv_all[c] = kv_ref[...]
     for other in range(ctxs):
 
@@ -428,7 +428,7 @@
         def _():
             att_copy(block, c).wait_recv()
 
-        out = lax.dot_general(att_all[block], ow[...], NN, preferred_element_type=jnp.float32)
+        out = lax.dot_general(att_all[block], ow[...], NT, preferred_element_type=jnp.float32)
         return jnp.concatenate(
             [out, jnp.zeros((rows, pad_cols - cols), jnp.float32)], axis=1
         )
@@ -543,7 +543,7 @@
         arrived(block, h ^ 1)
         arrived(block, h ^ 3)
 
-    gain = gain_ref[...]
+    gain = gain_ref[...].reshape(1, width)
     squares = []
     for row in range(ctxs):
         pieces = [h_all[block, row].astype(jnp.float32)[:, :cols] for block in range(ctxs)]
@@ -555,9 +555,9 @@
     inverse = lax.rsqrt(jnp.concatenate(squares, axis=0) / width + 1e-05)
     router_copy.wait()
     logits = lax.dot_general(
-        y_all[:, :width], router[...], NN, preferred_element_type=jnp.float32
+        y_all[:, :width], router[...], NT, preferred_element_type=jnp.float32
     ) * inverse
-    experts = router.shape[1]
+    experts = router.shape[0]
     expert_lane = lax.broadcasted_iota(jnp.int32, (all_rows, experts), 1).astype(jnp.float32)
     named = jnp.zeros((all_rows, experts), jnp.bool_)
     for k in range(topk):
@@ -627,23 +627,26 @@
             [jnp.zeros((cap, lead), jnp.bfloat16), rows_in[:, :width]], axis=1
         )
         factor = scale_ref[e][:1]
-        active = []
-        for u in range(2):
-            gate = factor * lax.dot_general(
-                wg[slot, u, :, :wide], rows_in, NT, preferred_element_type=jnp.float32
-            )
-            up = factor * lax.dot_general(
-                wg[slot, u, :, 2 * width - wide :],
-                shifted,
-                NT,
-                preferred_element_type=jnp.float32,
-            )
-            active.append(gate * jax.nn.sigmoid(1.702 * gate) * (up + 1.0))
+        gate = factor * lax.dot_general(
+            wg[slot, :, :, :wide].reshape(2 * units, wide),
+            rows_in,
+            NT,
+            preferred_element_type=jnp.float32,
+        )
+        up = factor * lax.dot_general(
+            wg[slot, :, :, 2 * width - wide :].reshape(2 * units, wide),
+            shifted,
+            NT,
+            preferred_element_type=jnp.float32,
+        )
+        active = gate * jax.nn.sigmoid(1.702 * gate) * (up + 1.0)
+        unit_rows[...] = jnp.concatenate(
+            [active, jnp.zeros((2 * units, LANES - cap), jnp.float32)], axis=1
+        )
         stacked = jnp.concatenate(
-            active + [jnp.zeros((packed - 2 * units, cap), jnp.float32)], axis=0
-        )
-        stacked = jnp.concatenate(
-            [stacked, jnp.zeros((packed, LANES - cap), jnp.float32)], axis=1
+            [unit_rows[pl.ds(u, units, stride=2), :] for u in range(2)]
+            + [jnp.zeros((packed - 2 * units, LANES), jnp.float32)],
+            axis=0,
         )
         act_all[h, e] = jnp.transpose(stacked)[:cap].astype(jnp.bfloat16)
         act_x(e).start()
@@ -769,9 +772,9 @@
             pltpu.VMEM((ctxs, seqs, tokens, keyvals.shape[3]), bf16),
             pltpu.VMEM((ctxs, 8, LANES), f32),
             pltpu.VMEM((seqs, tokens, cols), bf16),
-            pltpu.VMEM(out_weight.shape, bf16),
-            pltpu.VMEM(router.shape, bf16),
-            pltpu.VMEM((slots, 2, units, wide_w), bf16),
+            pltpu.VMEM(out_weight.shape[::-1], bf16),
+            pltpu.VMEM(router.shape[::-1], bf16),
+            pltpu.VMEM((slots, units, 2, wide_w), bf16),
             pltpu.VMEM(w_down.shape, bf16),
             pltpu.VMEM((ctxs, rows, q_cols), bf16),
             pltpu.VMEM((2, rows, pad_cols), bf16),
@@ -785,6 +788,7 @@
             pltpu.VMEM((all_rows, local_experts * LANES), bf16),
             pltpu.VMEM((local_experts * cap, wide), bf16),
             pltpu.VMEM((local_experts, 8, cap), f32),
+            pltpu.VMEM((2 * units, LANES), f32),
             pltpu.VMEM((4, local_experts, cap, packed), bf16),
             pltpu.VMEM((local_experts * LANES, pad_cols), bf16),
             pltpu.VMEM((ctxs, rows, pad_cols), bf16),
@@ -817,13 +821,13 @@
     )(
         queries,
         keyvals.reshape(seqs, tokens, keyvals.shape[3]),
-        ids,
+        jnp.transpose(ids, (0, 2, 1)),
         sinks,
-        gain.reshape(1, width),
+        gain,
         stream,
-        out_weight,
-        router,
-        w_gate_up,
+        out_weight.T,
+        router.T,
+        jnp.transpose(w_gate_up, (1, 0, 2)),
         w_down,
     )
 

time: 141 us -> 111 us (0.79)
  local copies, waits for them, and re-layouts: 32.2 us -> 1.62 us
    unnamed x5 -> x1, local copies, waits for them, and re-layouts: 30.9 us -> 1.62 us
where the time goes in v2:
time: 111 us; the launch traced here: 109 us
  Pallas kernels  108 us (97%)
  local copies, waits for them, and re-layouts  1.62 us (1%)
    pallas_call x1, Pallas kernels, layer_call(): pl.pallas_call(functools.partial(layer_kernel, sizes), out_shape=jax.Shap...  108 us

profile of v2, /device:TPU:0, one launch (start us, length us, event | category | flops | bytes accessed | tf_op | source)
XLA Modules:
  0.0 109.5 jit_solution(17846231557714955888)
XLA Ops:
  0.0 107.8 %shard_map.100 = bf16[2,64,720]{2,1,0:T(8,128)(2,1)} custom-call(bf16[2,64,512]{2,1,0:T(8,128)(2,1)} %q_ref.1, bf16[2,64,128]{2,1,0:T(8,128)(2,1)} %bitcast.8, s32[2,4,64]{2,1,0:T(4,128)} %bitcast.9, f32[8]{0:T(128)} %sink_ref.1, f32[2880]{0:T(1024)} %gain_ref.1, bf16[2,64,720]{2,1,0:T(8,128)(2,1)} %stream_ref.1, bf16[720,512]{1,0:T(8,128)(2,1)} %bitcast.6, ...), custom_call_target="tpu_custom_call" | custom-call | tf_op jit(solution)/shard_map/pallas_call | solution.py:765
  107.9 1.6 %copy.12 = bf16[2,64,720]{2,1,0:T(8,128)(2,1)} copy(bf16[2,64,720]{2,1,0:T(8,128)(2,1)} %shard_map.100) | data formatting | bytes 368640

commit v3 on v2

--- a/solution.py
+++ b/solution.py
@@ -169,22 +169,26 @@
 
 def layer_kernel(
     sizes,
-    q_ref,
-    kv_ref,
+    q_hbm,
+    kv_hbm,
     ids_ref,
     sink_ref,
-    gain_ref,
-    stream_ref,
+    gain_hbm,
+    stream_hbm,
     ow_hbm,
     router_hbm,
     wg_hbm,
     wd_hbm,
     out_ref,
+    q_ref,
+    gain_ref,
+    gains,
     kv_all,
     ids_all,
     stream_in,
     ow,
     router,
+    routers,
     wg,
     wd,
     att_all,
@@ -194,7 +198,10 @@
     x_out,
     x_in,
     h_all,
-    y_all,
+    y_ref,
+    square_ref,
+    logits_ref,
+    token_ref,
     pick,
     spread,
     xg,
@@ -204,6 +211,7 @@
     parts,
     rs_out,
     rs_in,
+    relay_in,
     local_sem,
     wg_sem,
     wd_sem,
@@ -225,11 +233,12 @@
     act_recv,
     rs_send,
     rs_recv,
+    relay_recv,
 ):
     seqs, tokens, rows, ctxs, width, cols, cap, local_experts, units, slots = sizes
     c, h, r = lax.axis_index("ctx"), lax.axis_index("head"), lax.axis_index("rep")
     all_rows = ctxs * rows
-    wide = y_all.shape[1]
+    wide = pl.cdiv(width, LANES) * LANES
     pad_cols = h_all.shape[3]
     core_dev, x_dev = (c, h ^ 1, r), (c, h ^ 2, r)
     partner = (h, c, r)
@@ -246,6 +255,9 @@
 
     ow_copy = pltpu.make_async_copy(ow_hbm, ow, local_sem.at[0])
     router_copy = pltpu.make_async_copy(router_hbm, router, local_sem.at[1])
+    q_copy = pltpu.make_async_copy(q_hbm, q_ref, local_sem.at[3])
+    kv_local = pltpu.make_async_copy(kv_hbm, kv_all.at[c], local_sem.at[4])
+    gain_copy = pltpu.make_async_copy(gain_hbm, gain_ref, local_sem.at[5])
 
     def wg_copy(e, slot):
         return pltpu.make_async_copy(
@@ -269,10 +281,13 @@
     def _():
         pl.semaphore_signal(barrier, inc=1, device_id=partner, device_id_type=MESH)
 
+    kv_local.start()
+    q_copy.start()
+    gain_copy.start()
+    router_copy.start()
     ow_copy.start()
     for e in range(min(slots, local_experts)):
         wg_copy(e, e).start()
-    router_copy.start()
     for e in range(local_experts):
         wd_copy(e).start()
     topk = ids_ref.shape[1]
@@ -280,7 +295,6 @@
     ids_all[c] = jnp.concatenate(
         [own_ids, jnp.full((8 - topk, rows), -1.0, jnp.float32)], axis=0
     )
-    kv_all[c] = kv_ref[...]
     for other in range(ctxs):
 
         @pl.when(other > c)
@@ -291,19 +305,16 @@
     pl.semaphore_wait(barrier, ctxs + 1 + (c != h).astype(jnp.int32))
 
     def kv_copy(src, dst):
-        return remote(
-            kv_all.at[src], kv_all.at[src], kv_send.at[dst], kv_recv.at[src], (dst, h, r)
-        )
+        return remote(kv_hbm, kv_all.at[src], kv_send.at[dst], kv_recv.at[src], (dst, h, r))
 
     def ids_copy(src, dst):
         return remote(
             ids_all.at[src], ids_all.at[src], ids_send.at[dst], ids_recv.at[src], (dst, h, r)
         )
 
-    def att_copy(src, dst):
-        return remote(
-            att_all.at[src], att_all.at[src], att_send.at[dst], att_recv.at[src], (dst, h, r)
-        )
+    def att_copy(src, dst, s):
+        part = att_all.at[src, pl.ds(s * tokens, tokens)]
+        return remote(part, part, att_send.at[dst, s], att_recv.at[src, s], (dst, h, r))
 
     for dst in range(ctxs):
 
@@ -312,9 +323,9 @@
             kv_copy(c, dst).start()
 
     stream_copy = remote(
-        stream_ref, stream_in, stream_send.at[0], stream_recv.at[0], partner
-    )
-    stream_local = pltpu.make_async_copy(stream_ref, stream_in, local_sem.at[2])
+        stream_hbm, stream_in, stream_send.at[0], stream_recv.at[0], partner
+    )
+    stream_local = pltpu.make_async_copy(stream_hbm, stream_in, local_sem.at[2])
 
     @pl.when(c != h)
     def _():
@@ -330,6 +341,8 @@
         def _():
             ids_copy(c, dst).start()
 
+    kv_local.wait()
+    q_copy.wait()
     for src in range(ctxs):
 
         @pl.when(src < c)
@@ -381,11 +394,11 @@
             att_all[c, s * tokens : (s + 1) * tokens, p * LANES : (p + 1) * LANES] = attended[
                 p * tokens : (p + 1) * tokens
             ]
-    for dst in range(ctxs):
-
-        @pl.when(dst != c)
-        def _():
-            att_copy(c, dst).start()
+        for dst in range(ctxs):
+
+            @pl.when(dst != c)
+            def _():
+                att_copy(c, dst, s).start()
 
     for src in range(ctxs):
 
@@ -418,35 +431,61 @@
     both = jnp.concatenate(
         [ids_row, slot_row, jnp.zeros((LANES - 8 - local_experts, all_rows), jnp.float32)], axis=0
     )
-    by_token = jnp.transpose(both)
+    token_ref[...] = jnp.transpose(both)
+    gain_copy.wait()
+    router_copy.wait()
+    gain = gain_ref[...].reshape(1, width)
+    for block in range(ctxs):
+        here = slice(block * cols, (block + 1) * cols)
+        gains[block] = jnp.concatenate(
+            [jnp.broadcast_to(gain[:, here], (8, cols)), jnp.zeros((8, pad_cols - cols), jnp.float32)],
+            axis=1,
+        )
+        routers[block] = jnp.concatenate(
+            [
+                router[:, here],
+                jnp.zeros((router.shape[0], pad_cols - cols), jnp.bfloat16),
+            ],
+            axis=1,
+        )
 
     ow_copy.wait()
     side, core = h // 2, lax.rem(h, 2)
 
-    def projected(block):
-        @pl.when(block != c)
-        def _():
-            att_copy(block, c).wait_recv()
-
-        out = lax.dot_general(att_all[block], ow[...], NT, preferred_element_type=jnp.float32)
-        return jnp.concatenate(
-            [out, jnp.zeros((rows, pad_cols - cols), jnp.float32)], axis=1
-        )
-
-    def core_copy(i):
-        return remote(core_out.at[i], core_in.at[i], core_send.at[i], core_recv.at[i], core_dev)
-
-    for i in range(2):
-        across = (1 - side) if i == 0 else side
-        core_out[i] = projected(2 * across + 1 - core).astype(jnp.bfloat16)
-        core_copy(i).start()
-    for i in range(2):
-        across = (1 - side) if i == 0 else side
-        keep[i] = projected(2 * across + core)
-    core_copy(0).wait_recv()
-    x_out[...] = (keep[0] + core_in[0].astype(jnp.float32)).astype(jnp.bfloat16)
-    x_copy = remote(x_out, x_in, x_send.at[0], x_recv.at[0], x_dev)
-    x_copy.start()
+    def widened(values):
+        extra = jnp.zeros((values.shape[0], pad_cols - cols), jnp.float32)
+        return jnp.concatenate([values, extra], axis=1)
+
+    def projected(blocks, s):
+        stacked = jnp.concatenate(
+            [att_all[block, s * tokens : (s + 1) * tokens] for block in blocks], axis=0
+        )
+        return widened(
+            lax.dot_general(stacked, ow[...], NT, preferred_element_type=jnp.float32)
+        )
+
+    def core_copy(s):
+        return remote(core_out.at[s], core_in.at[s], core_send.at[s], core_recv.at[s], core_dev)
+
+    def x_copy(s):
+        return remote(x_out.at[s], x_in.at[s], x_send.at[s], x_recv.at[s], x_dev)
+
+    for s in range(seqs):
+        for block in range(ctxs):
+
+            @pl.when(block != c)
+            def _():
+                att_copy(block, c, s).wait_recv()
+
+        across = (1 - side, side)
+        core_out[s] = projected([2 * to + 1 - core for to in across], s).astype(jnp.bfloat16)
+        core_copy(s).start()
+        keep[s] = projected([2 * to + core for to in across], s)
+        core_copy(s).wait_recv()
+        x_out[s] = (keep[s, :tokens] + core_in[s, :tokens].astype(jnp.float32)).astype(
+            jnp.bfloat16
+        )
+        x_copy(s).start()
 
     @pl.when(c != h)
     def _():
@@ -456,108 +495,209 @@
     def _():
         stream_local.wait()
 
-    core_copy(1).wait_recv()
-    turned_stream = stream_in[...].reshape(rows, cols).astype(jnp.float32)
-    kept = (
-        keep[1]
-        + core_in[1].astype(jnp.float32)
-        + jnp.concatenate(
-            [turned_stream, jnp.zeros((rows, pad_cols - cols), jnp.float32)], axis=1
-        )
-    )
-    x_copy.wait_recv()
-    h_all[c, h] = (kept + x_in[...].astype(jnp.float32)).astype(jnp.bfloat16)
-
-    def h_copy(way, block, row, device):
-        return remote(
-            h_all.at[block, row],
-            h_all.at[block, row],
-            h_send.at[way, block],
-            h_recv.at[block, row],
-            device,
-        )
-
-    def h_core(block, row):
-        return h_copy(jnp.where(row == h, 0, 1), block, row, core_dev)
-
-    def h_x(block):
-        return h_copy(2, block, h, x_dev)
-
-    def h_right(block):
-        return h_copy(3, block, h, (jnp.minimum(c + 1, ctxs - 1), h, r))
-
-    def h_left(block):
-        return h_copy(4, block, h, (jnp.maximum(c - 1, 0), h, r))
-
-    def arrived(block, row):
-        h_copy(0, block, row, core_dev).wait_recv()
-
-    h_x(c).start()
-
-    @pl.when(c < ctxs - 1)
-    def _():
-        h_right(c).start()
-
-    @pl.when(c > 0)
-    def _():
-        h_left(c).start()
-
-    h_core(c, h).start()
+    def h_copy(way, block, row, s, device):
+        part = h_all.at[block, row, pl.ds(s * tokens, tokens)]
+        return remote(part, part, h_send.at[way, block, s], h_recv.at[block, row, s], device)
+
+    def h_core(block, row, s):
+        return h_copy(jnp.where(row == h, 0, 1), block, row, s, core_dev)
+
+    def h_x(block, s):
+        return h_copy(2, block, h, s, x_dev)
+
+    def h_right(block, s):
+        return h_copy(3, block, h, s, (jnp.minimum(c + 1, ctxs - 1), h, r))
+
+    def h_left(block, s):
+        return h_copy(4, block, h, s, (jnp.maximum(c - 1, 0), h, r))
+
+    def arrived(block, row, s):
+        h_copy(0, block, row, s, core_dev).wait_recv()
+
+    for s in range(seqs):
+        kept = (
+            keep[s, tokens:]
+            + core_in[s, tokens:].astype(jnp.float32)
+            + widened(stream_in[s].astype(jnp.float32))
+        )
+        x_copy(s).wait_recv()
+        h_all[c, h, s * tokens : (s + 1) * tokens] = (
+            kept + x_in[s].astype(jnp.float32)
+        ).astype(jnp.bfloat16)
+        h_x(c, s).start()
+
+        @pl.when(c < ctxs - 1)
+        def _():
+            h_right(c, s).start()
+
+        @pl.when(c > 0)
+        def _():
+            h_left(c, s).start()
+
+        h_core(c, h, s).start()
+
+    square_ref[...] = jnp.zeros(square_ref.shape, jnp.float32)
+    logits_ref[...] = jnp.zeros(logits_ref.shape, jnp.float32)
+
+    def take(block):
+        for s in range(seqs):
+            arrived(block, h ^ 1, s)
+            arrived(block, h ^ 3, s)
+        for row in range(ctxs):
+            here = slice(row * rows, (row + 1) * rows)
+            piece = h_all[block, row].astype(jnp.float32)
+            y_ref[here, :] = (piece * gains[block][:1]).astype(jnp.bfloat16)
+            square = piece * piece
+            square_ref[here, :] += sum(
+                square[:, i : i + LANES] for i in range(0, pad_cols, LANES)
+            )
+        xg[block] = lax.dot_general(
+            pick[...], y_ref[...], NN, preferred_element_type=jnp.float32
+        ).astype(jnp.bfloat16)
+        logits_ref[...] += lax.dot_general(
+            y_ref[...], routers[block], NT, preferred_element_type=jnp.float32
+        )
+
     for d in range(1, ctxs + 1):
-
-        @pl.when(c - d >= 0)
-        def _():
-            arrived(c - d, h)
-
-            @pl.when(c < ctxs - 1)
+        for s in range(seqs):
+
+            @pl.when(c - d >= 0)
             def _():
-                h_right(c - d).start()
-
-            h_x(c - d).start()
-            h_core(c - d, h).start()
-
-        @pl.when(c + d < ctxs)
-        def _():
-            arrived(c + d, h)
-
-            @pl.when(c > 0)
+                arrived(c - d, h, s)
+
+                @pl.when(c < ctxs - 1)
+                def _():
+                    h_right(c - d, s).start()
+
+                h_x(c - d, s).start()
+                h_core(c - d, h, s).start()
+
+            @pl.when(c + d < ctxs)
             def _():
-                h_left(c + d).start()
-
-            h_x(c + d).start()
-            h_core(c + d, h).start()
+                arrived(c + d, h, s)
+
+                @pl.when(c > 0)
+                def _():
+                    h_left(c + d, s).start()
+
+                h_x(c + d, s).start()
+                h_core(c + d, h, s).start()
+
+            @pl.when(c - (d - 1) >= 0)
+            def _():
+                arrived(c - (d - 1), h ^ 2, s)
+                h_core(c - (d - 1), h ^ 2, s).start()
+
+            if d > 1:
+
+                @pl.when(c + (d - 1) < ctxs)
+                def _():
+                    arrived(c + (d - 1), h ^ 2, s)
+                    h_core(c + (d - 1), h ^ 2, s).start()
 
         @pl.when(c - (d - 1) >= 0)
         def _():
-            arrived(c - (d - 1), h ^ 2)
-            h_core(c - (d - 1), h ^ 2).start()
+            take(c - (d - 1))
 
         if d > 1:
 
             @pl.when(c + (d - 1) < ctxs)
             def _():
-                arrived(c + (d - 1), h ^ 2)
-                h_core(c + (d - 1), h ^ 2).start()
-
-    for block in range(ctxs):
-        arrived(block, h ^ 1)
-        arrived(block, h ^ 3)
-
-    gain = gain_ref[...].reshape(1, width)
-    squares = []
-    for row in range(ctxs):
-        pieces = [h_all[block, row].astype(jnp.float32)[:, :cols] for block in range(ctxs)]
-        squares.append(sum(jnp.sum(piece * piece, axis=1, keepdims=True) for piece in pieces))
-        flat = jnp.concatenate(pieces, axis=1) * gain
-        y_all[row * rows : (row + 1) * rows, :] = jnp.concatenate(
-            [flat, jnp.zeros((rows, wide - width), jnp.float32)], axis=1
-        ).astype(jnp.bfloat16)
-    inverse = lax.rsqrt(jnp.concatenate(squares, axis=0) / width + 1e-05)
-    router_copy.wait()
-    logits = lax.dot_general(
-        y_all[:, :width], router[...], NT, preferred_element_type=jnp.float32
-    ) * inverse
-    experts = router.shape[0]
+                take(c + (d - 1))
+
+    inverse = lax.rsqrt(jnp.sum(square_ref[...], axis=1, keepdims=True) / width + 1e-05)
+    square_ref[...] = jnp.broadcast_to(inverse, square_ref.shape)
+    inverse_row = jnp.transpose(square_ref[...])[:1]
+    first = inverse_row.astype(jnp.bfloat16)
+    rest = inverse_row - first.astype(jnp.float32)
+    second = rest.astype(jnp.bfloat16)
+    third = (rest - second.astype(jnp.float32)).astype(jnp.bfloat16)
+    in_parts = jnp.concatenate(
+        [part.astype(jnp.float32) for part in (first, second, third)]
+        + [jnp.zeros((5, all_rows), jnp.float32)],
+        axis=0,
+    ).astype(jnp.bfloat16)
+    for e in range(local_experts):
+        found = lax.dot_general(
+            in_parts, pick[e * cap : (e + 1) * cap, :], NT, preferred_element_type=jnp.float32
+        )
+        scale_ref[e] = jnp.broadcast_to(jnp.sum(found, axis=0, keepdims=True), (8, cap))
+
+    def act_core(shard, e):
+        return remote(
+            act_all.at[shard, e],
+            act_all.at[shard, e],
+            act_send.at[jnp.where(shard == h, 0, 1), e],
+            act_recv.at[shard, e],
+            core_dev,
+        )
+
+    def act_x(e):
+        return remote(
+            act_all.at[h, e], act_all.at[h, e], act_send.at[2, e], act_recv.at[h, e], x_dev
+        )
+
+    def act_arrived(shard, e):
+        remote(
+            act_all.at[shard, e],
+            act_all.at[shard, e],
+            act_send.at[0, e],
+            act_recv.at[shard, e],
+            core_dev,
+        ).wait_recv()
+
+    lead = wide - width
+    packed = act_all.shape[3]
+
+    @pl.loop(0, local_experts)
+    def _(e):
+        slot = lax.rem(e, slots)
+        wg_copy(e, slot).wait()
+        pieces = [
+            xg[block, pl.ds(pl.multiple_of(e * cap, cap), cap), :][:, :cols]
+            for block in range(ctxs)
+        ]
+        blank = [jnp.zeros((cap, lead), jnp.bfloat16)]
+        rows_in = jnp.concatenate(pieces + blank, axis=1)
+        shifted = jnp.concatenate(blank + pieces, axis=1)
+        factor = scale_ref[e][:1]
+        gate = factor * lax.dot_general(
+            wg[slot, :, :, :wide].reshape(2 * units, wide),
+            rows_in,
+            NT,
+            preferred_element_type=jnp.float32,
+        )
+        up = factor * lax.dot_general(
+            wg[slot, :, :, 2 * width - wide :].reshape(2 * units, wide),
+            shifted,
+            NT,
+            preferred_element_type=jnp.float32,
+        )
+        active = gate * jax.nn.sigmoid(1.702 * gate) * (up + 1.0)
+        unit_rows[...] = jnp.concatenate(
+            [active, jnp.zeros((2 * units, LANES - cap), jnp.float32)], axis=1
+        )
+        stacked = jnp.concatenate(
+            [unit_rows[pl.ds(u, units, stride=2), :] for u in range(2)]
+            + [jnp.zeros((packed - 2 * units, LANES), jnp.float32)],
+            axis=0,
+        )
+        act_all[h, e] = jnp.transpose(stacked)[:cap].astype(jnp.bfloat16)
+        act_x(e).start()
+        act_core(h, e).start()
+
+        @pl.when(e + slots < local_experts)
+        def _():
+            wg_copy(e + slots, slot).start()
+
+        @pl.when(e >= 2)
+        def _():
+            act_arrived(h ^ 2, e - 2)
+            act_core(h ^ 2, e - 2).start()
+
+    by_token = token_ref[...]
+    logits = logits_ref[...] * square_ref[:, :1]
+    experts = logits.shape[1]
     expert_lane = lax.broadcasted_iota(jnp.int32, (all_rows, experts), 1).astype(jnp.float32)
     named = jnp.zeros((all_rows, experts), jnp.bool_)
     for k in range(topk):
@@ -572,94 +712,6 @@
         spread[:, e * LANES : (e + 1) * LANES] = jnp.where(
             slot_lane == by_token[:, 8 + e : 9 + e], mix[:, e : e + 1], 0.0
         ).astype(jnp.bfloat16)
-
-    inverse_row = jnp.transpose(jnp.broadcast_to(inverse, (all_rows, LANES)))[:8]
-    first = inverse_row.astype(jnp.bfloat16)
-    rest = inverse_row - first.astype(jnp.float32)
-    second = rest.astype(jnp.bfloat16)
-    third = (rest - second.astype(jnp.float32)).astype(jnp.bfloat16)
-    for e in range(local_experts):
-        here = pick[e * cap : (e + 1) * cap, :]
-        scale_ref[e] = sum(
-            lax.dot_general(part, here, NT, preferred_element_type=jnp.float32)
-            for part in (first, second, third)
-        )
-
-    @pl.loop(0, wide // LANES)
-    def _(j):
-        at = pl.multiple_of(j * LANES, LANES)
-        xg[:, pl.ds(at, LANES)] = lax.dot_general(
-            pick[...], y_all[:, pl.ds(at, LANES)], NN, preferred_element_type=jnp.float32
-        ).astype(jnp.bfloat16)
-
-    def act_core(shard, e):
-        return remote(
-            act_all.at[shard, e],
-            act_all.at[shard, e],
-            act_send.at[jnp.where(shard == h, 0, 1), e],
-            act_recv.at[shard, e],
-            core_dev,
-        )
-
-    def act_x(e):
-        return remote(
-            act_all.at[h, e], act_all.at[h, e], act_send.at[2, e], act_recv.at[h, e], x_dev
-        )
-
-    def act_arrived(shard, e):
-        remote(
-            act_all.at[shard, e],
-            act_all.at[shard, e],
-            act_send.at[0, e],
-            act_recv.at[shard, e],
-            core_dev,
-        ).wait_recv()
-
-    lead = wide - width
-    packed = act_all.shape[3]
-
-    @pl.loop(0, local_experts)
-    def _(e):
-        slot = lax.rem(e, slots)
-        wg_copy(e, slot).wait()
-        rows_in = xg[pl.ds(pl.multiple_of(e * cap, cap), cap), :]
-        shifted = jnp.concatenate(
-            [jnp.zeros((cap, lead), jnp.bfloat16), rows_in[:, :width]], axis=1
-        )
-        factor = scale_ref[e][:1]
-        gate = factor * lax.dot_general(
-            wg[slot, :, :, :wide].reshape(2 * units, wide),
-            rows_in,
-            NT,
-            preferred_element_type=jnp.float32,
-        )
-        up = factor * lax.dot_general(
-            wg[slot, :, :, 2 * width - wide :].reshape(2 * units, wide),
-            shifted,
-            NT,
-            preferred_element_type=jnp.float32,
-        )
-        active = gate * jax.nn.sigmoid(1.702 * gate) * (up + 1.0)
-        unit_rows[...] = jnp.concatenate(
-            [active, jnp.zeros((2 * units, LANES - cap), jnp.float32)], axis=1
-        )
-        stacked = jnp.concatenate(
-            [unit_rows[pl.ds(u, units, stride=2), :] for u in range(2)]
-            + [jnp.zeros((packed - 2 * units, LANES), jnp.float32)],
-            axis=0,
-        )
-        act_all[h, e] = jnp.transpose(stacked)[:cap].astype(jnp.bfloat16)
-        act_x(e).start()
-        act_core(h, e).start()
-
-        @pl.when(e + slots < local_experts)
-        def _():
-            wg_copy(e + slots, slot).start()
-
-        @pl.when(e >= 2)
-        def _():
-            act_arrived(h ^ 2, e - 2)
-            act_core(h ^ 2, e - 2).start()
 
     for e in range(local_experts - 2, local_experts):
         act_arrived(h ^ 2, e)
@@ -694,15 +746,42 @@
             preferred_element_type=jnp.float32,
         )
 
-    for d in range(1, ctxs):
-        dst = lax.rem(c + d, ctxs)
-        rs_out[dst] = combined(dst).astype(jnp.bfloat16)
-        rs_copy(c, dst).start()
-    total = combined(c) + h_all[h, c].astype(jnp.float32)
-    for d in range(1, ctxs):
-        src = lax.rem(c + d, ctxs)
-        rs_copy(src, c).wait_recv()
-        total = total + rs_in[src].astype(jnp.float32)
+    outer = (c == 0) | (c == ctxs - 1)
+    far = ctxs - 1 - c
+    relay_dst = jnp.where(c == 0, 1, 2)
+    end_dst = jnp.where(c == 1, 3, 0)
+    relay_copy = remote(
+        rs_out.at[far], relay_in, rs_send.at[far], relay_recv.at[0], (relay_dst, h, r)
+    )
+
+    @pl.when(outer)
+    def _():
+        rs_out[far] = combined(far).astype(jnp.bfloat16)
+        relay_copy.start()
+        for dst in (ctxs - 1 - relay_dst, relay_dst):
+            rs_out[dst] = combined(dst).astype(jnp.bfloat16)
+            rs_copy(c, dst).start()
+
+    @pl.when(jnp.logical_not(outer))
+    def _():
+        for dst in (ctxs - 1 - c, ctxs - 1 - end_dst):
+            rs_out[dst] = combined(dst).astype(jnp.bfloat16)
+            rs_copy(c, dst).start()
+        ends = combined(end_dst)
+        relay_copy.wait_recv()
+        rs_out[end_dst] = (ends + relay_in[...].astype(jnp.float32)).astype(jnp.bfloat16)
+        rs_copy(c, end_dst).start()
+
+    keep[0] = combined(c) + h_all[h, c].astype(jnp.float32)
+    for src in range(ctxs):
+        sends_here = (src != c) & jnp.logical_not(outer & (src == far))
+
+        @pl.when(sends_here)
+        def _():
+            rs_copy(src, c).wait_recv()
+            keep[0] += rs_in[src].astype(jnp.float32)
+
+    total = keep[0]
     out_ref[...] = total[:, :cols].astype(jnp.bfloat16).reshape(out_ref.shape)
 
     for dst in range(ctxs):
@@ -714,28 +793,29 @@
         @pl.when(dst != c)
         def _():
             ids_copy(c, dst).wait_send()
-            att_copy(c, dst).wait_send()
+            for s in range(seqs):
+                att_copy(c, dst, s).wait_send()
             rs_copy(c, dst).wait_send()
 
     @pl.when(c != h)
     def _():
         stream_copy.wait_send()
 
-    x_copy.wait_send()
-    for i in range(2):
-        core_copy(i).wait_send()
-    for block in range(ctxs):
-        h_x(block).wait_send()
-        h_core(block, h).wait_send()
-        h_core(block, h ^ 2).wait_send()
-
-        @pl.when((c < ctxs - 1) & (block <= c))
-        def _():
-            h_right(block).wait_send()
-
-        @pl.when((c > 0) & (block >= c))
-        def _():
-            h_left(block).wait_send()
+    for s in range(seqs):
+        x_copy(s).wait_send()
+        core_copy(s).wait_send()
+        for block in range(ctxs):
+            h_x(block, s).wait_send()
+            h_core(block, h, s).wait_send()
+            h_core(block, h ^ 2, s).wait_send()
+
+            @pl.when((c < ctxs - 1) & (block <= c))
+            def _():
+                h_right(block, s).wait_send()
+
+            @pl.when((c > 0) & (block >= c))
+            def _():
+                h_left(block, s).wait_send()
 
     for e in range(local_experts):
         act_x(e).wait_send()
@@ -753,7 +833,6 @@
     local_experts = halves // 2
     all_rows = ctxs * rows
     cap = all_rows * 3 // 16
-    wide = pl.cdiv(width, LANES) * LANES
     pad_cols = pl.cdiv(cols, LANES) * LANES
     packed = pl.cdiv(2 * units, LANES) * LANES
     slots = min(4, local_experts)
@@ -765,35 +844,42 @@
     return pl.pallas_call(
         functools.partial(layer_kernel, sizes),
         out_shape=jax.ShapeDtypeStruct((seqs, tokens, cols), bf16),
-        in_specs=[vmem, vmem, vmem, pl.BlockSpec(memory_space=pltpu.SMEM), vmem, vmem]
-        + [hbm] * 4,
+        in_specs=[hbm, hbm, vmem, pl.BlockSpec(memory_space=pltpu.SMEM)] + [hbm] * 6,
         out_specs=vmem,
         scratch_shapes=[
+            pltpu.VMEM(queries.shape, bf16),
+            pltpu.VMEM(gain.shape, f32),
+            pltpu.VMEM((ctxs, 8, pad_cols), f32),
             pltpu.VMEM((ctxs, seqs, tokens, keyvals.shape[3]), bf16),
             pltpu.VMEM((ctxs, 8, LANES), f32),
             pltpu.VMEM((seqs, tokens, cols), bf16),
             pltpu.VMEM(out_weight.shape[::-1], bf16),
             pltpu.VMEM(router.shape[::-1], bf16),
+            pltpu.VMEM((ctxs, router.shape[1], pad_cols), bf16),
             pltpu.VMEM((slots, units, 2, wide_w), bf16),
             pltpu.VMEM(w_down.shape, bf16),
             pltpu.VMEM((ctxs, rows, q_cols), bf16),
-            pltpu.VMEM((2, rows, pad_cols), bf16),
-            pltpu.VMEM((2, rows, pad_cols), bf16),
-            pltpu.VMEM((2, rows, pad_cols), f32),
-            pltpu.VMEM((rows, pad_cols), bf16),
-            pltpu.VMEM((rows, pad_cols), bf16),
+            pltpu.VMEM((seqs, 2 * tokens, pad_cols), bf16),
+            pltpu.VMEM((seqs, 2 * tokens, pad_cols), bf16),
+            pltpu.VMEM((seqs, 2 * tokens, pad_cols), f32),
+            pltpu.VMEM((seqs, tokens, pad_cols), bf16),
+            pltpu.VMEM((seqs, tokens, pad_cols), bf16),
             pltpu.VMEM((ctxs, 4, rows, pad_cols), bf16),
-            pltpu.VMEM((all_rows, wide), bf16),
+            pltpu.VMEM((all_rows, pad_cols), bf16),
+            pltpu.VMEM((all_rows, LANES), f32),
+            pltpu.VMEM((all_rows, router.shape[1]), f32),
+            pltpu.VMEM((all_rows, LANES), f32),
             pltpu.VMEM((local_experts * cap, all_rows), bf16),
             pltpu.VMEM((all_rows, local_experts * LANES), bf16),
-            pltpu.VMEM((local_experts * cap, wide), bf16),
+            pltpu.VMEM((ctxs, local_experts * cap, pad_cols), bf16),
             pltpu.VMEM((local_experts, 8, cap), f32),
             pltpu.VMEM((2 * units, LANES), f32),
             pltpu.VMEM((4, local_experts, cap, packed), bf16),
             pltpu.VMEM((local_experts * LANES, pad_cols), bf16),
             pltpu.VMEM((ctxs, rows, pad_cols), bf16),
             pltpu.VMEM((ctxs, rows, pad_cols), bf16),
-            dma((3,)),
+            pltpu.VMEM((rows, pad_cols), bf16),
+            dma((6,)),
             dma((slots,)),
             dma((local_experts,)),
             dma((ctxs,)),
@@ -802,18 +888,19 @@
             dma((ctxs,)),
             dma((1,)),
             dma((1,)),
-            dma((ctxs,)),
-            dma((ctxs,)),
-            dma((2,)),
-            dma((2,)),
-            dma((1,)),
-            dma((1,)),
-            dma((5, ctxs)),
-            dma((ctxs, 4)),
+            dma((ctxs, seqs)),
+            dma((ctxs, seqs)),
+            dma((seqs,)),
+            dma((seqs,)),
+            dma((seqs,)),
+            dma((seqs,)),
+            dma((5, ctxs, seqs)),
+            dma((ctxs, 4, seqs)),
             dma((3, local_experts)),
             dma((4, local_experts)),
             dma((ctxs,)),
             dma((ctxs,)),
+            dma((1,)),
         ],
         compiler_params=pltpu.CompilerParams(
             vmem_limit_bytes=67043328, collective_id=0, has_side_effects=True

time: 111 us -> 95.9 us (0.86); the launches traced: 109 us -> 95.7 us
  Pallas kernels: 108 us -> 94 us
    pallas_call x1, Pallas kernels: 108 us -> 94 us  [layer_call(): pl.pallas_call(functools.partial(layer_kernel, sizes), out_shape=jax.Shap...]
where the time goes in v3:
time: 95.9 us; the launch traced here: 95.7 us
  Pallas kernels  94 us (98%)
  local copies, waits for them, and re-layouts  1.62 us (2%)
    pallas_call x1, Pallas kernels, layer_call(): pl.pallas_call(functools.partial(layer_kernel, sizes), out_shape=jax.Shap...  94 us

profile of v3, /device:TPU:0, one launch (start us, length us, event | category | flops | bytes accessed | tf_op | source)
XLA Modules:
  0.0 95.7 jit_solution(9804279978100967896)
XLA Ops:
  0.0 94.0 %shard_map.100 = bf16[2,64,720]{2,1,0:T(8,128)(2,1)} custom-call(bf16[2,64,512]{2,1,0:T(8,128)(2,1)} %q_hbm.1, bf16[2,64,128]{2,1,0:T(8,128)(2,1)} %bitcast.8, s32[2,4,64]{2,1,0:T(4,128)} %bitcast.9, f32[8]{0:T(128)} %sink_ref.1, f32[2880]{0:T(1024)} %gain_hbm.1, bf16[2,64,720]{2,1,0:T(8,128)(2,1)} %stream_hbm.1, bf16[720,512]{1,0:T(8,128)(2,1)} %bitcast.6, ...), custom_call_target="tpu_custom_call" | custom-call | tf_op jit(solution)/shard_map/pallas_call | solution.py:844
  94.1 1.6 %copy.12 = bf16[2,64,720]{2,1,0:T(8,128)(2,1)} copy(bf16[2,64,720]{2,1,0:T(8,128)(2,1)} %shard_map.100) | data formatting | bytes 368640

commit v4 on v3

--- a/solution.py
+++ b/solution.py
@@ -212,6 +212,8 @@
     rs_out,
     rs_in,
     relay_in,
+    hidden_ref,
+    total_ref,
     local_sem,
     wg_sem,
     wd_sem,
@@ -234,6 +236,7 @@
     rs_send,
     rs_recv,
     relay_recv,
+    onward_send,
 ):
     seqs, tokens, rows, ctxs, width, cols, cap, local_experts, units, slots = sizes
     c, h, r = lax.axis_index("ctx"), lax.axis_index("head"), lax.axis_index("rep")
@@ -316,6 +319,11 @@
         part = att_all.at[src, pl.ds(s * tokens, tokens)]
         return remote(part, part, att_send.at[dst, s], att_recv.at[src, s], (dst, h, r))
 
+    def att_onward(block, s):
+        part = att_all.at[block, pl.ds(s * tokens, tokens)]
+        end = (ctxs - 1 - block, h, r)
+        return remote(part, part, onward_send.at[s], att_recv.at[block, s], end)
+
     for dst in range(ctxs):
 
         @pl.when(dst > c)
@@ -326,14 +334,6 @@
         stream_hbm, stream_in, stream_send.at[0], stream_recv.at[0], partner
     )
     stream_local = pltpu.make_async_copy(stream_hbm, stream_in, local_sem.at[2])
-
-    @pl.when(c != h)
-    def _():
-        stream_copy.start()
-
-    @pl.when(c == h)
-    def _():
-        stream_local.start()
 
     for dst in range(ctxs):
 
@@ -396,9 +396,17 @@
             ]
         for dst in range(ctxs):
 
-            @pl.when(dst != c)
+            @pl.when((dst != c) & (lax.abs(dst - c) < ctxs - 1))
             def _():
                 att_copy(c, dst, s).start()
+
+    @pl.when(c != h)
+    def _():
+        stream_copy.start()
+
+    @pl.when(c == h)
+    def _():
+        stream_local.start()
 
     for src in range(ctxs):
 
@@ -471,11 +479,17 @@
         return remote(x_out.at[s], x_in.at[s], x_send.at[s], x_recv.at[s], x_dev)
 
     for s in range(seqs):
-        for block in range(ctxs):
+        for block in (0, ctxs - 1) + tuple(range(1, ctxs - 1)):
 
             @pl.when(block != c)
             def _():
                 att_copy(block, c, s).wait_recv()
+
+            if block in (0, ctxs - 1):
+
+                @pl.when(c == lax.abs(block - (ctxs - 2)))
+                def _():
+                    att_onward(block, s).start()
 
         across = (1 - side, side)
         core_out[s] = projected([2 * to + 1 - core for to in across], s).astype(jnp.bfloat16)
@@ -649,10 +663,7 @@
     lead = wide - width
     packed = act_all.shape[3]
 
-    @pl.loop(0, local_experts)
-    def _(e):
-        slot = lax.rem(e, slots)
-        wg_copy(e, slot).wait()
+    def activated(e, slot):
         pieces = [
             xg[block, pl.ds(pl.multiple_of(e * cap, cap), cap), :][:, :cols]
             for block in range(ctxs)
@@ -673,12 +684,14 @@
             NT,
             preferred_element_type=jnp.float32,
         )
-        active = gate * jax.nn.sigmoid(1.702 * gate) * (up + 1.0)
-        unit_rows[...] = jnp.concatenate(
+        return gate * jax.nn.sigmoid(1.702 * gate) * (up + 1.0)
+
+    def hand_out(e, i, active):
+        unit_rows[i] = jnp.concatenate(
             [active, jnp.zeros((2 * units, LANES - cap), jnp.float32)], axis=1
         )
         stacked = jnp.concatenate(
-            [unit_rows[pl.ds(u, units, stride=2), :] for u in range(2)]
+            [unit_rows[i, pl.ds(u, units, stride=2), :] for u in range(2)]
             + [jnp.zeros((packed - 2 * units, LANES), jnp.float32)],
             axis=0,
         )
@@ -686,14 +699,24 @@
         act_x(e).start()
         act_core(h, e).start()
 
-        @pl.when(e + slots < local_experts)
-        def _():
-            wg_copy(e + slots, slot).start()
-
-        @pl.when(e >= 2)
-        def _():
-            act_arrived(h ^ 2, e - 2)
-            act_core(h ^ 2, e - 2).start()
+    @pl.loop(0, local_experts // 2)
+    def _(pair):
+        both = [(2 * pair + i, lax.rem(2 * pair + i, slots)) for i in range(2)]
+        for e, slot in both:
+            wg_copy(e, slot).wait()
+        results = [activated(e, slot) for e, slot in both]
+        for i, (e, slot) in enumerate(both):
+            hand_out(e, i, results[i])
+
+            @pl.when(e + slots < local_experts)
+            def _():
+                wg_copy(e + slots, slot).start()
+
+        @pl.when(pair >= 1)
+        def _():
+            for e, slot in both:
+                act_arrived(h ^ 2, e - 2)
+                act_core(h ^ 2, e - 2).start()
 
     by_token = token_ref[...]
     logits = logits_ref[...] * square_ref[:, :1]
@@ -717,31 +740,15 @@
         act_arrived(h ^ 2, e)
         act_core(h ^ 2, e).start()
 
-    @pl.loop(0, local_experts)
-    def _(e):
-        wd_copy(e).wait()
-        act_arrived(h ^ 1, e)
-        act_arrived(h ^ 3, e)
-        total = None
-        for u in range(2):
-            hidden = jnp.concatenate(
-                [act_all[shard, e][:, u * units : (u + 1) * units] for shard in range(4)], axis=1
-            )
-            piece = lax.dot_general(
-                hidden, wd[2 * e + u], NN, preferred_element_type=jnp.float32
-            )
-            total = piece if total is None else total + piece
-        parts[pl.ds(pl.multiple_of(e * LANES, LANES), cap), :] = jnp.concatenate(
-            [total, jnp.zeros((cap, pad_cols - cols), jnp.float32)], axis=1
-        ).astype(jnp.bfloat16)
-
-    def rs_copy(src, dst):
-        return remote(rs_out.at[dst], rs_in.at[src], rs_send.at[dst], rs_recv.at[src], (dst, h, r))
-
-    def combined(block):
+    def rs_copy(src, dst, j):
+        return remote(
+            rs_out.at[dst, j], rs_in.at[src, j], rs_send.at[dst, j], rs_recv.at[src, j], (dst, h, r)
+        )
+
+    def combined(block, j):
         return lax.dot_general(
             spread[pl.ds(pl.multiple_of(block * rows, rows), rows), :],
-            parts[...],
+            parts[j],
             NN,
             preferred_element_type=jnp.float32,
         )
@@ -750,38 +757,84 @@
     far = ctxs - 1 - c
     relay_dst = jnp.where(c == 0, 1, 2)
     end_dst = jnp.where(c == 1, 3, 0)
-    relay_copy = remote(
-        rs_out.at[far], relay_in, rs_send.at[far], relay_recv.at[0], (relay_dst, h, r)
-    )
-
-    @pl.when(outer)
-    def _():
-        rs_out[far] = combined(far).astype(jnp.bfloat16)
-        relay_copy.start()
-        for dst in (ctxs - 1 - relay_dst, relay_dst):
-            rs_out[dst] = combined(dst).astype(jnp.bfloat16)
-            rs_copy(c, dst).start()
+
+    def relay_copy(j):
+        return remote(
+            rs_out.at[far, j],
+            relay_in.at[j],
+            rs_send.at[far, j],
+            relay_recv.at[j],
+            (relay_dst, h, r),
+        )
+
+    chunk = parts.shape[2]
+    chunks = parts.shape[0]
+    for j in range(chunks):
+        first_col = j * chunk
+        last_col = min(cols, first_col + chunk)
+
+        @pl.loop(0, local_experts)
+        def _(e):
+            if j == 0:
+                wd_copy(e).wait()
+                act_arrived(h ^ 1, e)
+                act_arrived(h ^ 3, e)
+                for u in range(2):
+                    hidden_ref[2 * e + u] = jnp.concatenate(
+                        [act_all[shard, e][:, u * units : (u + 1) * units] for shard in range(4)],
+                        axis=1,
+                    )
+            total = None
+            for u in range(2):
+                piece = lax.dot_general(
+                    hidden_ref[2 * e + u],
+                    wd[2 * e + u, :, first_col:last_col],
+                    NN,
+                    preferred_element_type=jnp.float32,
+                )
+                total = piece if total is None else total + piece
+            if last_col - first_col < chunk:
+                extra = jnp.zeros((cap, chunk - (last_col - first_col)), jnp.float32)
+                total = jnp.concatenate([total, extra], axis=1)
+            parts[j, pl.ds(pl.multiple_of(e * LANES, LANES), cap), :] = total.astype(jnp.bfloat16)
+
+        @pl.when(outer)
+        def _():
+            rs_out[far, j] = combined(far, j).astype(jnp.bfloat16)
+            relay_copy(j).start()
+            for dst in (ctxs - 1 - relay_dst, relay_dst):
+                rs_out[dst, j] = combined(dst, j).astype(jnp.bfloat16)
+                rs_copy(c, dst, j).start()
+
+        @pl.when(jnp.logical_not(outer))
+        def _():
+            for dst in (ctxs - 1 - c, ctxs - 1 - end_dst):
+                rs_out[dst, j] = combined(dst, j).astype(jnp.bfloat16)
+                rs_copy(c, dst, j).start()
 
     @pl.when(jnp.logical_not(outer))
     def _():
-        for dst in (ctxs - 1 - c, ctxs - 1 - end_dst):
-            rs_out[dst] = combined(dst).astype(jnp.bfloat16)
-            rs_copy(c, dst).start()
-        ends = combined(end_dst)
-        relay_copy.wait_recv()
-        rs_out[end_dst] = (ends + relay_in[...].astype(jnp.float32)).astype(jnp.bfloat16)
-        rs_copy(c, end_dst).start()
-
-    keep[0] = combined(c) + h_all[h, c].astype(jnp.float32)
-    for src in range(ctxs):
-        sends_here = (src != c) & jnp.logical_not(outer & (src == far))
-
-        @pl.when(sends_here)
-        def _():
-            rs_copy(src, c).wait_recv()
-            keep[0] += rs_in[src].astype(jnp.float32)
-
-    total = keep[0]
+        for j in range(chunks):
+            ends = combined(end_dst, j)
+            relay_copy(j).wait_recv()
+            rs_out[end_dst, j] = (ends + relay_in[j].astype(jnp.float32)).astype(jnp.bfloat16)
+            rs_copy(c, end_dst, j).start()
+
+    own = h_all[h, c].astype(jnp.float32)
+    for j in range(chunks):
+        here = slice(j * chunk, (j + 1) * chunk)
+        total_ref[:, here] = combined(c, j) + own[:, here]
+    for j in range(chunks):
+        here = slice(j * chunk, (j + 1) * chunk)
+        for src in (1, 2, 0, 3):
+            sends_here = (src != c) & jnp.logical_not(outer & (src == far))
+
+            @pl.when(sends_here)
+            def _():
+                rs_copy(src, c, j).wait_recv()
+                total_ref[:, here] += rs_in[src, j].astype(jnp.float32)
+
+    total = total_ref[...]
     out_ref[...] = total[:, :cols].astype(jnp.bfloat16).reshape(out_ref.shape)
 
     for dst in range(ctxs):
@@ -793,9 +846,18 @@
         @pl.when(dst != c)
         def _():
             ids_copy(c, dst).wait_send()
+            for j in range(chunks):
+                rs_copy(c, dst, j).wait_send()
+
+        @pl.when((dst != c) & (lax.abs(dst - c) < ctxs - 1))
+        def _():
             for s in range(seqs):
                 att_copy(c, dst, s).wait_send()
-            rs_copy(c, dst).wait_send()
+
+    @pl.when((c == 1) | (c == ctxs - 2))
+    def _():
+        for s in range(seqs):
+            att_onward(jnp.where(c == 1, ctxs - 1, 0), s).wait_send()
 
     @pl.when(c != h)
     def _():
@@ -833,9 +895,11 @@
     local_experts = halves // 2
     all_rows = ctxs * rows
     cap = all_rows * 3 // 16
-    pad_cols = pl.cdiv(cols, LANES) * LANES
+    pad_cols = pl.cdiv(cols, 2 * LANES) * 2 * LANES
     packed = pl.cdiv(2 * units, LANES) * LANES
     slots = min(4, local_experts)
+    chunk = 2 * LANES
+    chunks = pl.cdiv(cols, chunk)
     sizes = (seqs, tokens, rows, ctxs, width, cols, cap, local_experts, units, slots)
     bf16, f32 = jnp.bfloat16, jnp.float32
     dma = pltpu.SemaphoreType.DMA
@@ -873,12 +937,14 @@
             pltpu.VMEM((all_rows, local_experts * LANES), bf16),
             pltpu.VMEM((ctxs, local_experts * cap, pad_cols), bf16),
             pltpu.VMEM((local_experts, 8, cap), f32),
-            pltpu.VMEM((2 * units, LANES), f32),
+            pltpu.VMEM((2, 2 * units, LANES), f32),
             pltpu.VMEM((4, local_experts, cap, packed), bf16),
-            pltpu.VMEM((local_experts * LANES, pad_cols), bf16),
-            pltpu.VMEM((ctxs, rows, pad_cols), bf16),
-            pltpu.VMEM((ctxs, rows, pad_cols), bf16),
-            pltpu.VMEM((rows, pad_cols), bf16),
+            pltpu.VMEM((chunks, local_experts * LANES, chunk), bf16),
+            pltpu.VMEM((ctxs, chunks, rows, chunk), bf16),
+            pltpu.VMEM((ctxs, chunks, rows, chunk), bf16),
+            pltpu.VMEM((chunks, rows, chunk), bf16),
+            pltpu.VMEM((halves, cap, w_down.shape[1]), bf16),
+            pltpu.VMEM((rows, chunks * chunk), f32),
             dma((6,)),
             dma((slots,)),
             dma((local_experts,)),
@@ -898,9 +964,10 @@
             dma((ctxs, 4, seqs)),
             dma((3, local_experts)),
             dma((4, local_experts)),
-            dma((ctxs,)),
-            dma((ctxs,)),
-            dma((1,)),
+            dma((ctxs, chunks)),
+            dma((ctxs, chunks)),
+            dma((chunks,)),
+            dma((seqs,)),
         ],
         compiler_params=pltpu.CompilerParams(
             vmem_limit_bytes=67043328, collective_id=0, has_side_effects=True

time: 95.9 us -> 96.9 us (1.010)
  Pallas kernels: 94 us -> 95.1 us
    pallas_call x1, Pallas kernels: 94 us -> 95.1 us  [layer_call(): pl.pallas_call(functools.partial(layer_kernel, sizes), out_shape=jax.Shap...]
where the time goes in v4:
time: 96.9 us; the launch traced here: 96.7 us
  Pallas kernels  95.1 us (98%)
  local copies, waits for them, and re-layouts  1.62 us (2%)
    pallas_call x1, Pallas kernels, layer_call(): pl.pallas_call(functools.partial(layer_kernel, sizes), out_shape=jax.Shap...  95.1 us

profile of v4, /device:TPU:0, one launch (start us, length us, event | category | flops | bytes accessed | tf_op | source)
XLA Modules:
  0.0 96.7 jit_solution(11640385707758353982)
XLA Ops:
  0.0 95.1 %shard_map.100 = bf16[2,64,720]{2,1,0:T(8,128)(2,1)} custom-call(bf16[2,64,512]{2,1,0:T(8,128)(2,1)} %q_hbm.1, bf16[2,64,128]{2,1,0:T(8,128)(2,1)} %bitcast.8, s32[2,4,64]{2,1,0:T(4,128)} %bitcast.9, f32[8]{0:T(128)} %sink_ref.1, f32[2880]{0:T(1024)} %gain_hbm.1, bf16[2,64,720]{2,1,0:T(8,128)(2,1)} %stream_hbm.1, bf16[720,512]{1,0:T(8,128)(2,1)} %bitcast.6, ...), custom_call_target="tpu_custom_call" | custom-call | tf_op jit(solution)/shard_map/pallas_call | solution.py:908
  95.1 1.6 %copy.12 = bf16[2,64,720]{2,1,0:T(8,128)(2,1)} copy(bf16[2,64,720]{2,1,0:T(8,128)(2,1)} %shard_map.100) | data formatting | bytes 368640

commit v5 on v4

--- a/solution.py
+++ b/solution.py
@@ -335,6 +335,14 @@
     )
     stream_local = pltpu.make_async_copy(stream_hbm, stream_in, local_sem.at[2])
 
+    @pl.when(c != h)
+    def _():
+        stream_copy.start()
+
+    @pl.when(c == h)
+    def _():
+        stream_local.start()
+
     for dst in range(ctxs):
 
         @pl.when(dst != c)
@@ -400,14 +408,6 @@
             def _():
                 att_copy(c, dst, s).start()
 
-    @pl.when(c != h)
-    def _():
-        stream_copy.start()
-
-    @pl.when(c == h)
-    def _():
-        stream_local.start()
-
     for src in range(ctxs):
 
         @pl.when(src != c)
@@ -686,12 +686,12 @@
         )
         return gate * jax.nn.sigmoid(1.702 * gate) * (up + 1.0)
 
-    def hand_out(e, i, active):
-        unit_rows[i] = jnp.concatenate(
+    def hand_out(e, active):
+        unit_rows[...] = jnp.concatenate(
             [active, jnp.zeros((2 * units, LANES - cap), jnp.float32)], axis=1
         )
         stacked = jnp.concatenate(
-            [unit_rows[i, pl.ds(u, units, stride=2), :] for u in range(2)]
+            [unit_rows[pl.ds(u, units, stride=2), :] for u in range(2)]
             + [jnp.zeros((packed - 2 * units, LANES), jnp.float32)],
             axis=0,
         )
@@ -699,24 +699,20 @@
         act_x(e).start()
         act_core(h, e).start()
 
-    @pl.loop(0, local_experts // 2)
-    def _(pair):
-        both = [(2 * pair + i, lax.rem(2 * pair + i, slots)) for i in range(2)]
-        for e, slot in both:
-            wg_copy(e, slot).wait()
-        results = [activated(e, slot) for e, slot in both]
-        for i, (e, slot) in enumerate(both):
-            hand_out(e, i, results[i])
-
-            @pl.when(e + slots < local_experts)
-            def _():
-                wg_copy(e + slots, slot).start()
-
-        @pl.when(pair >= 1)
-        def _():
-            for e, slot in both:
-                act_arrived(h ^ 2, e - 2)
-                act_core(h ^ 2, e - 2).start()
+    @pl.loop(0, local_experts)
+    def _(e):
+        slot = lax.rem(e, slots)
+        wg_copy(e, slot).wait()
+        hand_out(e, activated(e, slot))
+
+        @pl.when(e + slots < local_experts)
+        def _():
+            wg_copy(e + slots, slot).start()
+
+        @pl.when(e >= 2)
+        def _():
+            act_arrived(h ^ 2, e - 2)
+            act_core(h ^ 2, e - 2).start()
 
     by_token = token_ref[...]
     logits = logits_ref[...] * square_ref[:, :1]
@@ -937,7 +933,7 @@
             pltpu.VMEM((all_rows, local_experts * LANES), bf16),
             pltpu.VMEM((ctxs, local_experts * cap, pad_cols), bf16),
             pltpu.VMEM((local_experts, 8, cap), f32),
-            pltpu.VMEM((2, 2 * units, LANES), f32),
+            pltpu.VMEM((2 * units, LANES), f32),
             pltpu.VMEM((4, local_experts, cap, packed), bf16),
             pltpu.VMEM((chunks, local_experts * LANES, chunk), bf16),
             pltpu.VMEM((ctxs, chunks, rows, chunk), bf16),

time: 96.9 us -> 94.8 us (0.978)
  Pallas kernels: 95.1 us -> 93 us
    pallas_call x1, Pallas kernels: 95.1 us -> 93 us  [layer_call(): pl.pallas_call(functools.partial(layer_kernel, sizes), out_shape=jax.Shap...]
where the time goes in v5:
time: 94.8 us; the launch traced here: 94.6 us
  Pallas kernels  93 us (98%)
  local copies, waits for them, and re-layouts  1.62 us (2%)
    pallas_call x1, Pallas kernels, layer_call(): pl.pallas_call(functools.partial(layer_kernel, sizes), out_shape=jax.Shap...  93 us

profile of v5, /device:TPU:0, one launch (start us, length us, event | category | flops | bytes accessed | tf_op | source)
XLA Modules:
  0.0 94.6 jit_solution(10570995872093636797)
XLA Ops:
  0.0 93.0 %shard_map.100 = bf16[2,64,720]{2,1,0:T(8,128)(2,1)} custom-call(bf16[2,64,512]{2,1,0:T(8,128)(2,1)} %q_hbm.1, bf16[2,64,128]{2,1,0:T(8,128)(2,1)} %bitcast.8, s32[2,4,64]{2,1,0:T(4,128)} %bitcast.9, f32[8]{0:T(128)} %sink_ref.1, f32[2880]{0:T(1024)} %gain_hbm.1, bf16[2,64,720]{2,1,0:T(8,128)(2,1)} %stream_hbm.1, bf16[720,512]{1,0:T(8,128)(2,1)} %bitcast.6, ...), custom_call_target="tpu_custom_call" | custom-call | tf_op jit(solution)/shard_map/pallas_call | solution.py:904
  93.0 1.6 %copy.12 = bf16[2,64,720]{2,1,0:T(8,128)(2,1)} copy(bf16[2,64,720]{2,1,0:T(8,128)(2,1)} %shard_map.100) | data formatting | bytes 368640

commit v6 on v5

--- a/solution.py
+++ b/solution.py
@@ -335,6 +335,12 @@
     )
     stream_local = pltpu.make_async_copy(stream_hbm, stream_in, local_sem.at[2])
 
+    for dst in range(ctxs):
+
+        @pl.when(dst != c)
+        def _():
+            ids_copy(c, dst).start()
+
     @pl.when(c != h)
     def _():
         stream_copy.start()
@@ -342,12 +348,6 @@
     @pl.when(c == h)
     def _():
         stream_local.start()
-
-    for dst in range(ctxs):
-
-        @pl.when(dst != c)
-        def _():
-            ids_copy(c, dst).start()
 
     kv_local.wait()
     q_copy.wait()

time: 94.8 us -> 94.8 us (level)
  no operation moved by 1% of the time
where the time goes in v6:
time: 94.8 us; the launch traced here: 94.6 us
  Pallas kernels  93 us (98%)
  local copies, waits for them, and re-layouts  1.62 us (2%)
    pallas_call x1, Pallas kernels, layer_call(): pl.pallas_call(functools.partial(layer_kernel, sizes), out_shape=jax.Shap...  93 us

profile of v6, /device:TPU:0, one launch (start us, length us, event | category | flops | bytes accessed | tf_op | source)
XLA Modules:
  0.0 94.6 jit_solution(17272898649148549118)
XLA Ops:
  0.0 93.0 %shard_map.100 = bf16[2,64,720]{2,1,0:T(8,128)(2,1)} custom-call(bf16[2,64,512]{2,1,0:T(8,128)(2,1)} %q_hbm.1, bf16[2,64,128]{2,1,0:T(8,128)(2,1)} %bitcast.8, s32[2,4,64]{2,1,0:T(4,128)} %bitcast.9, f32[8]{0:T(128)} %sink_ref.1, f32[2880]{0:T(1024)} %gain_hbm.1, bf16[2,64,720]{2,1,0:T(8,128)(2,1)} %stream_hbm.1, bf16[720,512]{1,0:T(8,128)(2,1)} %bitcast.6, ...), custom_call_target="tpu_custom_call" | custom-call | tf_op jit(solution)/shard_map/pallas_call | solution.py:904
  93.0 1.6 %copy.12 = bf16[2,64,720]{2,1,0:T(8,128)(2,1)} copy(bf16[2,64,720]{2,1,0:T(8,128)(2,1)} %shard_map.100) | data formatting | bytes 368640
